TPU v7x, 32 devices: a whole 2x2x4 slice. The times are simulated.
32 devices in a mesh: groups: 2 (over x), segment: 4 (over z), head: 4 (over y, core).
Axes of the slice: x: 2, y: 2, z: 4, core: 2. Of those that a mesh axis runs over, the one named last changes fastest.
Arguments:
- hidden_in: bfloat16 [2048, 3072], P(('groups', 'segment'), 'head'), parts along dimension 0, may hold values from -6 to 6
- latent_in: bfloat16 [2048, 3072], P(('groups', 'segment'), 'head'), parts along dimension 0, may hold values from -6 to 6
- key_values: bfloat16 [8, 2, 1024, 3072], P(('groups', 'segment'), None, None, 'head'), parts along dimension 0, may hold values from -162 to 162
- qkv_weight: bfloat16 [4, 3072, 3, 3072], P('segment', None, None, 'head'), may hold values from -0.109375 to 0.109375
- out_weight: bfloat16 [4, 3072, 3072], P('segment', 'head'), may hold values from -0.109375 to 0.109375
- modulation: float32 [4, 16, 3, 3072], P('segment'), may hold values from -1.5 to 1.5
- step_sizes: float32 [16], replicated, may hold values from 0.25 to 2
- patch_order: int32 [8], P('groups'), parts along dimension 0, may hold values from 0 to 3, each once
- tick_patch: int32 [8, 4], P('groups'), parts along dimension 0, may hold values from 0 to 3
- step_ids: int32 [8, 4], P('groups'), parts along dimension 0, may hold values from 0 to 15
Outputs:
- out_hidden: bfloat16 [2048, 3072], P(('groups', 'segment'), 'head'), parts along dimension 0
- out_latent: bfloat16 [2048, 3072], P(('groups', 'segment'), 'head'), parts along dimension 0
There are 2 independent parts, one for each index of `groups`. A program takes and returns all parts, laid end to end along the dimension named above; an argument that names none is the same for every part. Nothing has to cross between parts.
All inputs are finite; a program needn't handle non-finite values.
Results may differ from a plain program's by a relative error of at most 0.028.
Values may be sent and summed in bfloat16 or wider, within the bound.
No kernel may reach another device: no remote copies, remote signals or barrier semaphores. Data moves between devices by JAX's collectives and lax.ppermute only.
A program may use at most 128 MiB of HBM per device.

v0:
```python
import functools

import jax
import jax.numpy as jnp
from jax import lax
from jax.experimental import pallas as pl
from jax.experimental.pallas import tpu as pltpu
from jax.sharding import PartitionSpec as P


HEAD_DIM = 64
LANES = 128
CHUNKS = 2
VMEM_BYTES = 12 << 20

IN_VMEM = pl.BlockSpec(memory_space=pltpu.VMEM)
ANYWHERE = pl.BlockSpec(memory_space=pl.ANY)


def shifted(value, axis, steps):
    count = lax.axis_size(axis)
    pairs = [(source, (source + steps) % count) for source in range(count)]
    return lax.ppermute(value, axis, pairs)


def swapped(value, axis, bit):
    return lax.ppermute(value, axis, [(i, i ^ bit) for i in range(lax.axis_size(axis))])


def position(axis):
    return lax.axis_index(axis).astype(jnp.int32)


def entry(row, index):
    row = row.astype(jnp.float32)
    hit = lax.broadcasted_iota(jnp.int32, row.shape, 1) == index
    return jnp.sum(jnp.where(hit, row, jnp.zeros_like(row)))


def whole(row, index):
    return entry(row, index).astype(jnp.int32)


def preload_kernel(weight, kept, sem):
    copy = pltpu.make_async_copy(weight, kept, sem)
    copy.start()
    copy.wait()


def preload(weight):
    return pl.pallas_call(
        preload_kernel,
        out_shape=pltpu.VMEM(weight.shape, weight.dtype),
        in_specs=[pl.BlockSpec(memory_space=pltpu.HBM)],
        out_specs=IN_VMEM,
        scratch_shapes=[pltpu.SemaphoreType.DMA],
        compiler_params=pltpu.CompilerParams(vmem_limit_bytes=VMEM_BYTES),
        cost_estimate=pl.CostEstimate(flops=0, bytes_accessed=4 * weight.size, transcendentals=0),
        name="preload",
    )(weight)


def project_kernel(width, tick, step_ids, x0, x1, x2, x3, mods, weight, queries, fresh, normed):
    me, segment = position("head"), position("segment")
    step = whole(step_ids[tick : tick + 1, :], segment)
    shares = (x0, x1, x2, x3)
    rows = x0.shape[0]
    features = len(shares) * width
    total = jnp.zeros((rows, 1), jnp.float32)
    for share in shares:
        total += jnp.sum(share[...].astype(jnp.float32), axis=-1, keepdims=True)
    center = total / features
    squares = jnp.zeros((rows, 1), jnp.float32)
    for share in shares:
        centered = share[...].astype(jnp.float32) - center
        squares += jnp.sum(centered * centered, axis=-1, keepdims=True)
    inverse = lax.rsqrt(squares / features + 1e-06)
    for j, share in enumerate(shares):
        at = pl.multiple_of((me ^ j) * width, width)
        centered = share[...].astype(jnp.float32) - center
        shift = mods[0, pl.ds(step, 1), pl.ds(at, width)]
        scale = mods[1, pl.ds(step, 1), pl.ds(at, width)]
        normed[:, pl.ds(at, width)] = (centered * inverse * (1.0 + scale) + shift).astype(
            jnp.bfloat16
        )
    queries[...] = jnp.dot(
        normed[...], weight[0], preferred_element_type=jnp.float32
    ).astype(jnp.bfloat16)

    @pl.loop(0, fresh.shape[0])
    def _(i):
        fresh[i] = jnp.dot(
            normed[...], weight[i + 1], preferred_element_type=jnp.float32
        ).astype(jnp.bfloat16)


def project(tick, step_ids, shares, mods, weight):
    rows, width = shares[0].shape
    return pl.pallas_call(
        functools.partial(project_kernel, width, tick),
        out_shape=(
            jax.ShapeDtypeStruct((rows, width), jnp.bfloat16),
            jax.ShapeDtypeStruct((2, rows, width), jnp.bfloat16),
        ),
        in_specs=[IN_VMEM] * 7,
        out_specs=(IN_VMEM,) * 2,
        scratch_shapes=[pltpu.VMEM((rows, 4 * width), jnp.bfloat16)],
        compiler_params=pltpu.CompilerParams(vmem_limit_bytes=VMEM_BYTES),
        cost_estimate=pl.CostEstimate(
            flops=2 * rows * 12 * width * width, bytes_accessed=14 * rows * width, transcendentals=0
        ),
        name="project",
    )(step_ids, *shares, mods, weight)


def attend_kernel(tick, chunks, extra, *refs):
    tick_patch, patch_order, old, weight = refs[:4]
    queries, fresh = refs[4 : 4 + 2 * chunks : 2], refs[5 : 4 + 2 * chunks : 2]
    far, heads, cache, even, odd = refs[4 + 2 * chunks + extra :]
    me, segment = position("head"), position("segment")
    patch = whole(patch_order[...], whole(tick_patch[tick : tick + 1, :], segment))
    rows, width = heads.shape

    @pl.loop(0, cache.shape[1] // rows)
    def _(block):
        cut = pl.ds(pl.multiple_of(block * rows, rows), rows)
        cache[:, cut, :] = old[:, cut, :]

    start = 0
    for part in fresh:
        at = pl.multiple_of(patch * rows + start, 16)
        cache[:, pl.ds(at, part.shape[1]), :] = part[...]
        start += part.shape[1]
    low = lax.broadcasted_iota(jnp.int32, (rows, LANES), 1) < HEAD_DIM
    zero = jnp.zeros((rows, LANES), jnp.bfloat16)
    ones = jnp.ones((cache.shape[1], LANES), jnp.bfloat16)

    def columns(pair):
        return pl.ds(pl.multiple_of(pair * LANES, LANES), LANES)

    def score(pair, scores):
        cols = columns(pair)
        query = jnp.concatenate([q[:, cols] for q in queries], axis=0) * jnp.bfloat16(
            HEAD_DIM**-0.5
        )
        both = jnp.concatenate(
            [jnp.where(low, query, zero), jnp.where(low, zero, query)], axis=0
        )
        scores[...] = lax.dot_general(
            both,
            cache[0, :, cols],
            (((1,), (1,)), ((), ())),
            preferred_element_type=jnp.float32,
        )

    def mix(pair, scores):
        cols = columns(pair)
        highest = jnp.max(scores[...], axis=-1, keepdims=True)
        expo = jnp.exp(scores[...] - highest).astype(jnp.bfloat16)
        mixed = jnp.dot(
            expo,
            jnp.concatenate([cache[1, :, cols], ones], axis=1),
            preferred_element_type=jnp.float32,
        )
        out = mixed[:, :LANES] / mixed[:, LANES:]
        heads[:, cols] = jnp.where(low, out[:rows], out[rows:]).astype(jnp.bfloat16)

    pairs = width // LANES
    score(0, even)

    @pl.loop(0, pairs // 2)
    def _(i):
        score(2 * i + 1, odd)
        mix(2 * i, even)
        score(jnp.minimum(2 * i + 2, pairs - 1), even)
        mix(2 * i + 1, odd)

    if pairs % 2:
        mix(pairs - 1, even)
    at = pl.multiple_of((me ^ 3) * width, width)
    far[...] = jnp.dot(
        heads[...], weight[:, pl.ds(at, width)], preferred_element_type=jnp.float32
    ).astype(jnp.bfloat16)


def attend(tick, plan, fresh, cache, weight, arrived, final):
    rows = sum(queries.shape[0] for queries, _ in fresh)
    _, tokens, width = cache.shape
    out = jax.ShapeDtypeStruct((rows, width), jnp.bfloat16)
    kept = jax.ShapeDtypeStruct(cache.shape, cache.dtype)
    return pl.pallas_call(
        functools.partial(attend_kernel, tick, len(fresh), len(arrived)),
        out_shape=(out, out) + (() if final else (kept,)),
        in_specs=[IN_VMEM] * (4 + 2 * len(fresh)) + [ANYWHERE] * len(arrived),
        out_specs=(IN_VMEM,) * (2 if final else 3),
        scratch_shapes=([pltpu.VMEM(cache.shape, cache.dtype)] if final else [])
        + [pltpu.VMEM((2 * rows, tokens), jnp.float32)] * 2,
        compiler_params=pltpu.CompilerParams(vmem_limit_bytes=VMEM_BYTES),
        cost_estimate=pl.CostEstimate(
            flops=2 * rows * width * (8 * tokens + 2 * width),
            bytes_accessed=14 * rows * width,
            transcendentals=rows * tokens * width // HEAD_DIM,
        ),
        name="attend",
    )(*plan, cache, weight, *[array for part in fresh for array in part], *arrived)


def output_kernel(heads, weight, out):
    me = position("head")
    width = heads.shape[1]

    @pl.loop(0, out.shape[0])
    def _(j):
        at = pl.multiple_of((me ^ j) * width, width)
        out[j] = jnp.dot(
            heads[...], weight[:, pl.ds(at, width)], preferred_element_type=jnp.float32
        ).astype(jnp.bfloat16)


def output(heads, weight):
    return pl.pallas_call(
        output_kernel,
        out_shape=jax.ShapeDtypeStruct((3,) + heads.shape, heads.dtype),
        in_specs=[IN_VMEM] * 2,
        out_specs=IN_VMEM,
        compiler_params=pltpu.CompilerParams(vmem_limit_bytes=VMEM_BYTES),
        cost_estimate=pl.CostEstimate(
            flops=6 * heads.size * heads.shape[1], bytes_accessed=6 * heads.size, transcendentals=0
        ),
        name="output",
    )(heads, weight)


def update_kernel(
    tick, start, step_ids, step_sizes, own, side, arrived, hidden, latent, mods, sent, advanced
):
    me, segment = position("head"), position("segment")
    rows, width = hidden.shape
    step = whole(step_ids[tick : tick + 1, :], segment)
    cut = pl.ds(start, rows)
    attended = (
        own[cut, :].astype(jnp.float32)
        + side[cut, :].astype(jnp.float32)
        + arrived[...].astype(jnp.float32)
    )
    at = pl.multiple_of(me * width, width)
    gate = 1.0 + mods[2, pl.ds(step, 1), pl.ds(at, width)]
    updated = (hidden[...].astype(jnp.float32) + gate * attended).astype(jnp.bfloat16)
    sent[...] = updated
    if advanced is not None:
        moved = (
            latent[cut, :].astype(jnp.float32) + entry(step_sizes[...], step) * updated.astype(jnp.float32)
        ).astype(jnp.bfloat16)
        advanced[...] = moved
        is_last = segment == lax.axis_size("segment") - 1

        @pl.when(is_last)
        def _():
            sent[...] = moved


def update(tick, start, tables, own, side, arrived, hidden, latent, mods):
    out = jax.ShapeDtypeStruct(hidden.shape, hidden.dtype)
    if latent is None:

        def body(*refs):
            update_kernel(tick, start, *refs[:6], None, *refs[6:8], None)

        arrays, outs = (own, side, arrived, hidden, mods), 1
    else:
        body = functools.partial(update_kernel, tick, start)
        arrays, outs = (own, side, arrived, hidden, latent, mods), 2
    return pl.pallas_call(
        body,
        out_shape=(out,) * outs,
        in_specs=[IN_VMEM] * (2 + len(arrays)),
        out_specs=(IN_VMEM,) * outs,
        compiler_params=pltpu.CompilerParams(vmem_limit_bytes=VMEM_BYTES),
        cost_estimate=pl.CostEstimate(
            flops=8 * hidden.size, bytes_accessed=16 * hidden.size, transcendentals=0
        ),
        name="update",
    )(*tables, *arrays)


def finish_kernel(cuts, count, step_ids, step_sizes, latent, *refs):
    segment = position("segment")
    last = lax.axis_size("segment") - 1
    parts = refs[: len(cuts)]
    kept = refs[len(cuts) : 2 * len(cuts)]
    moved = refs[2 * len(cuts) : 2 * len(cuts) + count]
    out_hidden, out_latent = refs[2 * len(cuts) + count :]
    for cut, part, piece in zip(cuts, parts, kept):
        out_hidden[cut, :] = part[...]
        out_latent[cut, :] = piece[...]
    for k, array in enumerate(moved):

        @pl.when(segment == last - 1 - k)
        def _():
            out_latent[...] = array[...]

    @pl.when(segment == 0)
    def _():
        step_size = entry(step_sizes[...], whole(step_ids[step_ids.shape[0] - 1 :, :], last))
        for cut, part in zip(cuts, parts):
            advanced = (
                latent[cut, :].astype(jnp.float32) + step_size * part[...].astype(jnp.float32)
            ).astype(jnp.bfloat16)
            out_hidden[cut, :] = advanced
            out_latent[cut, :] = advanced


def finish(cuts, tables, latent, parts, kept, moved):
    out = jax.ShapeDtypeStruct(latent.shape, latent.dtype)
    arrays = (latent, *parts, *kept, *moved)
    return pl.pallas_call(
        functools.partial(finish_kernel, cuts, len(moved)),
        out_shape=(out, out),
        in_specs=[IN_VMEM] * (2 + len(arrays)),
        out_specs=(IN_VMEM, IN_VMEM),
        compiler_params=pltpu.CompilerParams(vmem_limit_bytes=VMEM_BYTES),
        name="finish",
    )(*tables, *arrays)


def local_fast(
    hidden_in,
    latent_in,
    key_values,
    qkv_weight,
    out_weight,
    modulation,
    step_sizes,
    patch_order,
    tick_patch,
    step_ids,
):
    last = lax.axis_size("segment") - 1
    ticks = tick_patch.shape[0]
    rows = hidden_in.shape[0]
    weight = jnp.transpose(qkv_weight[0], (1, 0, 2))
    mods = jnp.transpose(modulation[0], (1, 0, 2))
    projection = out_weight[0]
    weight = preload(weight)
    cache = key_values[0]
    plan = (tick_patch, patch_order.reshape(1, -1))
    steps = (step_ids, step_sizes.reshape(1, -1))

    step_rows = rows // CHUNKS
    cuts = [slice(c * step_rows, (c + 1) * step_rows) for c in range(CHUNKS)]
    hidden = [hidden_in[cut] for cut in cuts]
    latents = {0: latent_in}
    kept, moved = [], []
    done = None
    for k in range(ticks):
        if done is not None:
            moved.append(lax.ppermute(done, "segment", [(last, last + 1 - k)]))
            done = None
        if k + 1 < last:
            latents[k + 1] = lax.ppermute(latent_in, "segment", [(last - k - 1, last)])
        fresh = []
        for part in hidden:
            across = swapped(part, "head", 2)
            beside = swapped(part, "head", 1)
            if fresh:
                across, _ = lax.optimization_barrier((across, fresh[-1][0]))
            corner = swapped(across, "head", 1)
            fresh.append(
                project(k, step_ids, (part, beside, across, corner), mods, weight)
            )
        arrived = moved[:-1]
        far, heads, *rest = attend(k, plan, fresh, cache, projection, arrived, k == ticks - 1)
        if rest:
            cache = rest[0]
        far_in = swapped(far, "head", 1)
        own, side, near = output(heads, projection)
        side_in = swapped(side, "head", 1)
        sums = [
            (near[cut].astype(jnp.float32) + far_in[cut].astype(jnp.float32)).astype(jnp.bfloat16)
            for cut in cuts
        ]
        crossed = []
        for c in range(CHUNKS):
            crossed.append(swapped(sums[c], "head", 2))
        advanced_parts = []
        sent = []
        for c, part in enumerate(hidden):
            latent = latents[k] if k < last else None
            onward, *advanced = update(
                k, cuts[c].start, steps, own, side_in, crossed[c], part, latent, mods
            )
            advanced_parts += advanced
            sent.append(shifted(onward, "segment", 1))
        hidden = sent
        if k == 0:
            kept = advanced_parts
        elif k < last:
            done = jnp.concatenate(advanced_parts, axis=0)
    return finish(cuts, steps, latent_in, hidden, kept, moved)


def normalize(hidden_rows, shift_vec, scale_vec):
    values_f32 = hidden_rows.astype(jnp.float32)
    center = jnp.mean(values_f32, axis=-1, keepdims=True)
    centered = values_f32 - center
    variance = jnp.mean(centered * centered, axis=-1, keepdims=True)
    return (centered * lax.rsqrt(variance + 1e-06) * (1.0 + scale_vec) + shift_vec).astype(
        jnp.bfloat16
    )


def pick_value(table_row, index_value):
    positions = jnp.arange(table_row.shape[0], dtype=jnp.int32)
    return jnp.sum(jnp.where(positions == index_value, table_row, jnp.zeros_like(table_row)))


def local_general(
    hidden_in,
    latent_in,
    key_values,
    qkv_weight,
    out_weight,
    modulation,
    step_sizes,
    patch_order,
    tick_patch,
    step_ids,
):
    segment_index = lax.axis_index("segment")
    last_segment = lax.axis_size("segment") - 1
    local_width = out_weight.shape[1]
    model_width = out_weight.shape[2]
    column = lax.axis_index("head") * local_width
    heads_here = local_width // HEAD_DIM
    patch_rows = hidden_in.shape[0]
    weights_local = qkv_weight[0].reshape(model_width, 3 * local_width)
    projection = out_weight[0]
    step_table = modulation[0]
    layer_cache = key_values[0]
    tokens = layer_cache.shape[1]
    is_last = segment_index == last_segment
    part_hidden, part_latent = (hidden_in, latent_in)
    for tick_number in range(tick_patch.shape[0]):
        position = pick_value(tick_patch[tick_number], segment_index)
        patch_index = pick_value(patch_order, position)
        step_index = pick_value(step_ids[tick_number], segment_index)
        mods = lax.dynamic_index_in_dim(step_table, step_index, 0, keepdims=False)
        step_size = pick_value(step_sizes, step_index)
        patch_index, mods, step_size = (patch_index, mods, step_size)
        full_hidden = lax.all_gather(part_hidden, "head", axis=1, tiled=True)
        current_cache = layer_cache
        normed = normalize(full_hidden, mods[0], mods[1])
        projected = jnp.dot(normed, weights_local, preferred_element_type=jnp.float32)
        projected = projected.astype(jnp.bfloat16).reshape(patch_rows, 3, local_width)
        fresh_rows = jnp.stack([projected[:, 1], projected[:, 2]])
        zero_index = jnp.zeros((), jnp.int32)
        current_cache = lax.dynamic_update_slice(
            current_cache, fresh_rows, (zero_index, patch_index * patch_rows, zero_index)
        )
        queries = projected[:, 0].reshape(patch_rows, heads_here, HEAD_DIM)
        cached_keys = current_cache[0].reshape(tokens, heads_here, HEAD_DIM)
        cached_values = current_cache[1].reshape(tokens, heads_here, HEAD_DIM)
        scores = jnp.einsum(
            "phd,lhd->hpl", queries, cached_keys, preferred_element_type=jnp.float32
        ) * HEAD_DIM ** (-0.5)
        highest = jnp.max(scores, axis=-1, keepdims=True)
        expo = jnp.exp(scores - highest)
        attention = (expo / jnp.sum(expo, axis=-1, keepdims=True)).astype(jnp.bfloat16)
        head_out = jnp.einsum(
            "hpl,lhd->phd", attention, cached_values, preferred_element_type=jnp.float32
        )
        head_out = head_out.astype(jnp.bfloat16).reshape(patch_rows, local_width)
        partial_value = jnp.dot(head_out, projection, preferred_element_type=jnp.float32)
        partial_value, layer_cache = (partial_value, current_cache)
        attended = lax.psum_scatter(
            partial_value.astype(jnp.bfloat16), "head", scatter_dimension=1, tiled=True
        ).astype(jnp.float32)
        gate_cols = lax.dynamic_slice_in_dim(mods[2], column, local_width, 0)
        updated = (part_hidden.astype(jnp.float32) + (1.0 + gate_cols) * attended).astype(
            jnp.bfloat16
        )
        advanced = (
            part_latent.astype(jnp.float32) + step_size * updated.astype(jnp.float32)
        ).astype(jnp.bfloat16)
        send_hidden = jnp.where(is_last, advanced, updated)
        send_latent = jnp.where(is_last, advanced, part_latent)
        part_hidden, part_latent = shifted((send_hidden, send_latent), "segment", 1)
    return (part_hidden, part_latent)


def solution(mesh):
    shape = mesh.shape

    def local(*args):
        hidden_in, ticks = args[0], args[8].shape[0]
        fits = (
            shape["head"] == 4
            and hidden_in.shape[1] % LANES == 0
            and hidden_in.shape[0] % (16 * CHUNKS) == 0
            and ticks == shape["segment"]
            and ticks > 1
        )
        return local_fast(*args) if fits else local_general(*args)

    return jax.shard_map(
        local,
        mesh=mesh,
        in_specs=(
            P(("groups", "segment"), "head"),
            P(("groups", "segment"), "head"),
            P(("groups", "segment"), None, None, "head"),
            P("segment", None, None, "head"),
            P("segment", "head", None),
            P("segment", None, None, None),
            P(),
            P("groups"),
            P("groups", None),
            P("groups", None),
        ),
        out_specs=(P(("groups", "segment"), "head"), P(("groups", "segment"), "head")),
        check_vma=False,
    )
```

profile of v0, /device:TPU:0, one launch (start us, length us, event | category | flops | bytes accessed | tf_op | source)
XLA Modules:
  0.0 189.2 jit_solution(17666361331920529750)
XLA Ops:
  1.7 3.1 %collective-permute-start.1 = (bf16[128,768]{1,0:T(8,128)(2,1)S(1)}, bf16[128,768]{1,0:T(8,128)(2,1)S(1)}, u32[]{:S(2)}, u32[]{:S(2)}) collective-permute-start(bf16[128,768]{1,0:T(8,128)(2,1)S(1)} %get-tuple-element.105.x0.hidden), channel_id=1, source_target_pairs={{0,2},{1,3},{2,0},{3,1},{4,6},{5,7},{6,4},{7,5},{8,10},{9,11},{10,... | collective-permute-start | bytes 589832 | tf_op jit(solution)/shard_map/ppermute | solution.py:27
  4.7 4.9 %collective-permute-done.1.x2 = bf16[128,768]{1,0:T(8,128)(2,1)S(1)} collective-permute-done((bf16[128,768]{1,0:T(8,128)(2,1)S(1)}, bf16[128,768]{1,0:T(8,128)(2,1)S(1)}, u32[]{:S(2)}, u32[]{:S(2)}) %collective-permute-start.1) | collective-permute-done | bytes 196640 | tf_op jit(solution)/shard_map/ppermute | solution.py:27
  11.6 5.0 %copy-done.1 = bf16[1,3072,3,768]{3,1,2,0:T(8,128)(2,1)S(1)} copy-done((bf16[1,3072,3,768]{3,1,2,0:T(8,128)(2,1)S(1)}, bf16[1,3072,3,768]{3,1,2,0:T(8,128)(2,1)}, u32[]{:S(2)}) %copy-start.1) | copy-done | bytes 14155800
  17.7 3.2 %project.8 = (bf16[128,768]{1,0:T(8,128)(2,1)S(1)}, bf16[2,128,768]{2,1,0:T(8,128)(2,1)S(1)}) custom-call(s32[4,4]{1,0:T(4,128)S(1)} %copy-done.3, bf16[128,768]{1,0:T(8,128)(2,1)S(1)} %get-tuple-element.105.x0.hidden, bf16[128,768]{1,0:T(8,128)(2,1)S(1)} %collective-permute-done.x1, bf16[128,768]{1,0:T(8,128)(2,1)S(1)} %collective-permute-done.1.x2, ...), custom_call_target="tpu_custom_call" | custom-call | flops 1811939328 | bytes 1376256 | tf_op jit(solution)/shard_map/project/pallas_call | solution.py:99
  22.5 3.2 %project.9 = (bf16[128,768]{1,0:T(8,128)(2,1)S(1)}, bf16[2,128,768]{2,1,0:T(8,128)(2,1)S(1)}) custom-call(s32[4,4]{1,0:T(4,128)S(1)} %copy-done.3, bf16[128,768]{1,0:T(8,128)(2,1)S(1)} %get-tuple-element.104.x0.hidden, bf16[128,768]{1,0:T(8,128)(2,1)S(1)} %collective-permute-done.3.x1, bf16[128,768]{1,0:T(8,128)(2,1)S(1)} %collective-permute-done.4.x2, ...), custom_call_target="tpu_custom_call" | custom-call | flops 1811939328 | bytes 1376256 | tf_op jit(solution)/shard_map/project/pallas_call | solution.py:99
  25.7 5.6 %attend.4 = (bf16[256,768]{1,0:T(8,128)(2,1)S(1)}, bf16[256,768]{1,0:T(8,128)(2,1)S(1)}, bf16[2,1024,768]{2,1,0:T(8,128)(2,1)S(1)}) custom-call(s32[4,4]{1,0:T(4,128)S(1)} %copy-done.6, s32[1,4]{1,0:T(1,128)S(1)} %bitcast.103, bf16[2,1024,768]{2,1,0:T(8,128)(2,1)S(1)} %bitcast.102, bf16[768,3072]{1,0:T(8,128)(2,1)S(1)} %bitcast.84, ...), custom_call_target="tpu_custom_call" | custom-call | flops 3825205248 | bytes 2752512 | tf_op jit(solution)/shard_map/attend/pallas_call | solution.py:191
  35.0 5.8 %collective-permute-done.8.arrived = bf16[128,768]{1,0:T(8,128)(2,1)S(1)} collective-permute-done((bf16[128,768]{1,0:T(8,128)(2,1)S(1)}, bf16[128,768]{1,0:T(8,128)(2,1)S(1)}, u32[]{:S(2)}, u32[]{:S(2)}) %collective-permute-start.8) | collective-permute-done | bytes 196640 | tf_op jit(solution)/shard_map/ppermute | solution.py:27
  43.3 6.0 %collective-permute-done.9.x0.hidden = bf16[128,768]{1,0:T(8,128)(2,1)S(1)} collective-permute-done((bf16[128,768]{1,0:T(8,128)(2,1)S(1)}, bf16[128,768]{1,0:T(8,128)(2,1)S(1)}, u32[]{:S(2)}, u32[]{:S(2)}) %collective-permute-start.9) | collective-permute-done | bytes 196640 | tf_op jit(solution)/shard_map/ppermute | solution.py:23
  51.0 4.0 %collective-permute-done.11.x2 = bf16[128,768]{1,0:T(8,128)(2,1)S(1)} collective-permute-done((bf16[128,768]{1,0:T(8,128)(2,1)S(1)}, bf16[128,768]{1,0:T(8,128)(2,1)S(1)}, u32[]{:S(2)}, u32[]{:S(2)}) %collective-permute-start.11) | collective-permute-done | bytes 196640 | tf_op jit(solution)/shard_map/ppermute | solution.py:27
  55.0 2.9 %collective-permute-done.14.x0.hidden = bf16[128,768]{1,0:T(8,128)(2,1)S(1)} collective-permute-done((bf16[128,768]{1,0:T(8,128)(2,1)S(1)}, bf16[128,768]{1,0:T(8,128)(2,1)S(1)}, u32[]{:S(2)}, u32[]{:S(2)}) %collective-permute-start.14) | collective-permute-done | bytes 196640 | tf_op jit(solution)/shard_map/ppermute | solution.py:23
  59.4 3.2 %project.10 = (bf16[128,768]{1,0:T(8,128)(2,1)S(1)}, bf16[2,128,768]{2,1,0:T(8,128)(2,1)S(1)}) custom-call(s32[4,4]{1,0:T(4,128)S(1)} %copy-done.3, bf16[128,768]{1,0:T(8,128)(2,1)S(1)} %collective-permute-done.9.x0.hidden, bf16[128,768]{1,0:T(8,128)(2,1)S(1)} %collective-permute-done.10.x1, bf16[128,768]{1,0:T(8,128)(2,1)S(1)} %collective-permute-done.11.x2, ...), custom_call_target="tpu_custom_call" | custom-call | flops 1811939328 | bytes 1376256 | tf_op jit(solution)/shard_map/project/pallas_call | solution.py:99
  65.0 3.2 %project.11 = (bf16[128,768]{1,0:T(8,128)(2,1)S(1)}, bf16[2,128,768]{2,1,0:T(8,128)(2,1)S(1)}) custom-call(s32[4,4]{1,0:T(4,128)S(1)} %copy-done.3, bf16[128,768]{1,0:T(8,128)(2,1)S(1)} %collective-permute-done.14.x0.hidden, bf16[128,768]{1,0:T(8,128)(2,1)S(1)} %collective-permute-done.15.x1, bf16[128,768]{1,0:T(8,128)(2,1)S(1)} %collective-permute-done.16.x2, ...), custom_call_target="tpu_custom_call" | custom-call | flops 1811939328 | bytes 1376256 | tf_op jit(solution)/shard_map/project/pallas_call | solution.py:99
  68.2 5.6 %attend.5 = (bf16[256,768]{1,0:T(8,128)(2,1)S(1)}, bf16[256,768]{1,0:T(8,128)(2,1)S(1)}, bf16[2,1024,768]{2,1,0:T(8,128)(2,1)S(1)}) custom-call(s32[4,4]{1,0:T(4,128)S(1)} %copy-done.6, s32[1,4]{1,0:T(1,128)S(1)} %bitcast.104, bf16[2,1024,768]{2,1,0:T(8,128)(2,1)S(1)} %get-tuple-element.50.refs_2_, bf16[768,3072]{1,0:T(8,128)(2,1)S(1)} %bitcast.86, ...), custom_call_target="tpu_custom_call" | custom-call | flops 3825205248 | bytes 2752512 | tf_op jit(solution)/shard_map/attend/pallas_call | solution.py:191
  78.4 5.4 %collective-permute-done.20.arrived = bf16[128,768]{1,0:T(8,128)(2,1)S(1)} collective-permute-done((bf16[128,768]{1,0:T(8,128)(2,1)S(1)}, bf16[128,768]{1,0:T(8,128)(2,1)S(1)}, u32[]{:S(2)}, u32[]{:S(2)}) %collective-permute-start.20) | collective-permute-done | bytes 196640 | tf_op jit(solution)/shard_map/ppermute | solution.py:27
  85.8 7.0 %collective-permute-done.22.x0.hidden = bf16[128,768]{1,0:T(8,128)(2,1)S(1)} collective-permute-done((bf16[128,768]{1,0:T(8,128)(2,1)S(1)}, bf16[128,768]{1,0:T(8,128)(2,1)S(1)}, u32[]{:S(2)}, u32[]{:S(2)}) %collective-permute-start.22) | collective-permute-done | bytes 196640 | tf_op jit(solution)/shard_map/ppermute | solution.py:23
  94.7 3.8 %collective-permute-done.24.x2 = bf16[128,768]{1,0:T(8,128)(2,1)S(1)} collective-permute-done((bf16[128,768]{1,0:T(8,128)(2,1)S(1)}, bf16[128,768]{1,0:T(8,128)(2,1)S(1)}, u32[]{:S(2)}, u32[]{:S(2)}) %collective-permute-start.24) | collective-permute-done | bytes 196640 | tf_op jit(solution)/shard_map/ppermute | solution.py:27
  98.5 3.3 %collective-permute-done.27.x0.hidden = bf16[128,768]{1,0:T(8,128)(2,1)S(1)} collective-permute-done((bf16[128,768]{1,0:T(8,128)(2,1)S(1)}, bf16[128,768]{1,0:T(8,128)(2,1)S(1)}, u32[]{:S(2)}, u32[]{:S(2)}) %collective-permute-start.27) | collective-permute-done | bytes 196640 | tf_op jit(solution)/shard_map/ppermute | solution.py:23
  102.9 3.2 %project.12 = (bf16[128,768]{1,0:T(8,128)(2,1)S(1)}, bf16[2,128,768]{2,1,0:T(8,128)(2,1)S(1)}) custom-call(s32[4,4]{1,0:T(4,128)S(1)} %copy-done.3, bf16[128,768]{1,0:T(8,128)(2,1)S(1)} %collective-permute-done.22.x0.hidden, bf16[128,768]{1,0:T(8,128)(2,1)S(1)} %collective-permute-done.23.x1, bf16[128,768]{1,0:T(8,128)(2,1)S(1)} %collective-permute-done.24.x2, ...), custom_call_target="tpu_custom_call" | custom-call | flops 1811939328 | bytes 1376256 | tf_op jit(solution)/shard_map/project/pallas_call | solution.py:99
  109.0 3.2 %project.13 = (bf16[128,768]{1,0:T(8,128)(2,1)S(1)}, bf16[2,128,768]{2,1,0:T(8,128)(2,1)S(1)}) custom-call(s32[4,4]{1,0:T(4,128)S(1)} %copy-done.3, bf16[128,768]{1,0:T(8,128)(2,1)S(1)} %collective-permute-done.27.x0.hidden, bf16[128,768]{1,0:T(8,128)(2,1)S(1)} %collective-permute-done.28.x1, bf16[128,768]{1,0:T(8,128)(2,1)S(1)} %collective-permute-done.29.x2, ...), custom_call_target="tpu_custom_call" | custom-call | flops 1811939328 | bytes 1376256 | tf_op jit(solution)/shard_map/project/pallas_call | solution.py:99
  112.2 5.6 %attend.6 = (bf16[256,768]{1,0:T(8,128)(2,1)S(1)}, bf16[256,768]{1,0:T(8,128)(2,1)S(1)}, bf16[2,1024,768]{2,1,0:T(8,128)(2,1)S(1)}) custom-call(s32[4,4]{1,0:T(4,128)S(1)} %copy-done.6, s32[1,4]{1,0:T(1,128)S(1)} %bitcast.105, bf16[2,1024,768]{2,1,0:T(8,128)(2,1)S(1)} %get-tuple-element.60.refs_2_, bf16[768,3072]{1,0:T(8,128)(2,1)S(1)} %bitcast.88, ...), custom_call_target="tpu_custom_call" | custom-call | flops 3825205248 | bytes 2752512 | tf_op jit(solution)/shard_map/attend/pallas_call | solution.py:191
  122.0 5.8 %collective-permute-done.33.arrived = bf16[128,768]{1,0:T(8,128)(2,1)S(1)} collective-permute-done((bf16[128,768]{1,0:T(8,128)(2,1)S(1)}, bf16[128,768]{1,0:T(8,128)(2,1)S(1)}, u32[]{:S(2)}, u32[]{:S(2)}) %collective-permute-start.33) | collective-permute-done | bytes 196640 | tf_op jit(solution)/shard_map/ppermute | solution.py:27
  128.1 1.8 collective-permute-start.35
  130.9 6.2 %collective-permute-done.35.x0.refs_5_ = bf16[128,768]{1,0:T(8,128)(2,1)S(1)} collective-permute-done((bf16[128,768]{1,0:T(8,128)(2,1)S(1)}, bf16[128,768]{1,0:T(8,128)(2,1)S(1)}, u32[]{:S(2)}, u32[]{:S(2)}) %collective-permute-start.35) | collective-permute-done | bytes 196640 | tf_op jit(solution)/shard_map/ppermute | solution.py:23
  138.7 4.2 %collective-permute-done.37.x2 = bf16[128,768]{1,0:T(8,128)(2,1)S(1)} collective-permute-done((bf16[128,768]{1,0:T(8,128)(2,1)S(1)}, bf16[128,768]{1,0:T(8,128)(2,1)S(1)}, u32[]{:S(2)}, u32[]{:S(2)}) %collective-permute-start.37) | collective-permute-done | bytes 196640 | tf_op jit(solution)/shard_map/ppermute | solution.py:27
  142.9 3.2 %collective-permute-done.40.x0.refs_5_ = bf16[128,768]{1,0:T(8,128)(2,1)S(1)} collective-permute-done((bf16[128,768]{1,0:T(8,128)(2,1)S(1)}, bf16[128,768]{1,0:T(8,128)(2,1)S(1)}, u32[]{:S(2)}, u32[]{:S(2)}) %collective-permute-start.40) | collective-permute-done | bytes 196640 | tf_op jit(solution)/shard_map/ppermute | solution.py:23
  148.1 3.2 %project.14 = (bf16[128,768]{1,0:T(8,128)(2,1)S(1)}, bf16[2,128,768]{2,1,0:T(8,128)(2,1)S(1)}) custom-call(s32[4,4]{1,0:T(4,128)S(1)} %copy-done.3, bf16[128,768]{1,0:T(8,128)(2,1)S(1)} %collective-permute-done.35.x0.refs_5_, bf16[128,768]{1,0:T(8,128)(2,1)S(1)} %collective-permute-done.36.x1, bf16[128,768]{1,0:T(8,128)(2,1)S(1)} %collective-permute-done.37.x2, ...), custom_call_target="tpu_custom_call" | custom-call | flops 1811939328 | bytes 1376256 | tf_op jit(solution)/shard_map/project/pallas_call | solution.py:99
  153.1 3.2 %project.15 = (bf16[128,768]{1,0:T(8,128)(2,1)S(1)}, bf16[2,128,768]{2,1,0:T(8,128)(2,1)S(1)}) custom-call(s32[4,4]{1,0:T(4,128)S(1)} %copy-done.3, bf16[128,768]{1,0:T(8,128)(2,1)S(1)} %collective-permute-done.40.x0.refs_5_, bf16[128,768]{1,0:T(8,128)(2,1)S(1)} %collective-permute-done.41.x1, bf16[128,768]{1,0:T(8,128)(2,1)S(1)} %collective-permute-done.42.x2, ...), custom_call_target="tpu_custom_call" | custom-call | flops 1811939328 | bytes 1376256 | tf_op jit(solution)/shard_map/project/pallas_call | solution.py:99
  156.4 5.6 %attend.7 = (bf16[256,768]{1,0:T(8,128)(2,1)S(1)}, bf16[256,768]{1,0:T(8,128)(2,1)S(1)}) custom-call(s32[4,4]{1,0:T(4,128)S(1)} %copy-done.6, s32[1,4]{1,0:T(1,128)S(1)} %bitcast.106, bf16[2,1024,768]{2,1,0:T(8,128)(2,1)S(1)} %get-tuple-element.70.refs_2_, bf16[768,3072]{1,0:T(8,128)(2,1)S(1)} %bitcast.90, bf16[128,768]{1,0:T(8,128)(2,1)S(1)} %get-tuple-element.74.refs_4_, ...), custom_call_target="tpu_custom_call" | custom-call | flops 3825205248 | bytes 2752512 | tf_op jit(solution)/shard_map/attend/pallas_call | solution.py:191
  167.2 5.0 %collective-permute-done.49.refs_4_ = bf16[128,768]{1,0:T(8,128)(2,1)S(1)} collective-permute-done((bf16[128,768]{1,0:T(8,128)(2,1)S(1)}, bf16[128,768]{1,0:T(8,128)(2,1)S(1)}, u32[]{:S(2)}, u32[]{:S(2)}) %collective-permute-start.49) | collective-permute-done | bytes 196640 | tf_op jit(solution)/shard_map/ppermute | solution.py:27
  172.4 3.1 %collective-permute-done.47.refs_4_ = bf16[128,768]{1,0:T(8,128)(2,1)S(1)} collective-permute-done((bf16[128,768]{1,0:T(8,128)(2,1)S(1)}, bf16[128,768]{1,0:T(8,128)(2,1)S(1)}, u32[]{:S(2)}, u32[]{:S(2)}) %collective-permute-start.47) | collective-permute-done | bytes 196640 | tf_op jit(solution)/shard_map/ppermute | solution.py:27
  175.8 8.8 %collective-permute-done.50.refs_1_ = bf16[128,768]{1,0:T(8,128)(2,1)S(1)} collective-permute-done((bf16[128,768]{1,0:T(8,128)(2,1)S(1)}, bf16[128,768]{1,0:T(8,128)(2,1)S(1)}, u32[]{:S(2)}, u32[]{:S(2)}) %collective-permute-start.50) | collective-permute-done | bytes 196640 | tf_op jit(solution)/shard_map/ppermute | solution.py:23
  184.6 3.3 %collective-permute-done.48.refs_0_ = bf16[128,768]{1,0:T(8,128)(2,1)S(1)} collective-permute-done((bf16[128,768]{1,0:T(8,128)(2,1)S(1)}, bf16[128,768]{1,0:T(8,128)(2,1)S(1)}, u32[]{:S(2)}, u32[]{:S(2)}) %collective-permute-start.48) | collective-permute-done | bytes 196640 | tf_op jit(solution)/shard_map/ppermute | solution.py:23
  (130 shorter events, 47.9 us)
Async XLA Ops:
  1.7 8.0 %collective-permute-start.1 = (bf16[128,768]{1,0:T(8,128)(2,1)S(1)}, bf16[128,768]{1,0:T(8,128)(2,1)S(1)}, u32[]{:S(2)}, u32[]{:S(2)}) collective-permute-start(bf16[128,768]{1,0:T(8,128)(2,1)S(1)} %get-tuple-element.105.x0.hidden), channel_id=1, source_target_pairs={{0,2},{1,3},{2,0},{3,1},{4,6},{5,7},{6,4},{7,5},{8,10},{9,11},{10,... | collective-permute-start | bytes 589832 | tf_op jit(solution)/shard_map/ppermute | solution.py:27
  4.7 12.9 %collective-permute-start = (bf16[128,768]{1,0:T(8,128)(2,1)S(1)}, bf16[128,768]{1,0:T(8,128)(2,1)S(1)}, u32[]{:S(2)}, u32[]{:S(2)}) collective-permute-start(bf16[128,768]{1,0:T(8,128)(2,1)S(1)} %get-tuple-element.105.x0.hidden), channel_id=1, source_target_pairs={{0,1},{1,0},{2,3},{3,2},{4,5},{5,4},{6,7},{7,6},{8,9},{9,8},{10,11... | collective-permute-start | bytes 589832 | tf_op jit(solution)/shard_map/ppermute | solution.py:27
  9.6 8.0 %collective-permute-start.2 = (bf16[128,768]{1,0:T(8,128)(2,1)S(1)}, bf16[128,768]{1,0:T(8,128)(2,1)S(1)}, u32[]{:S(2)}, u32[]{:S(2)}) collective-permute-start(bf16[128,768]{1,0:T(8,128)(2,1)S(1)} %collective-permute-done.1.x2), channel_id=1, source_target_pairs={{0,1},{1,0},{2,3},{3,2},{4,5},{5,4},{6,7},{7,6},{8,9},{9,8},{10,11... | collective-permute-start | bytes 589832 | tf_op jit(solution)/shard_map/ppermute | solution.py:27
  9.6 11.3 %collective-permute-start.4 = (bf16[128,768]{1,0:T(8,128)(2,1)S(1)}, bf16[128,768]{1,0:T(8,128)(2,1)S(1)}, u32[]{:S(2)}, u32[]{:S(2)}) collective-permute-start(bf16[128,768]{1,0:T(8,128)(2,1)S(1)} %get-tuple-element.104.x0.hidden), channel_id=1, source_target_pairs={{0,2},{1,3},{2,0},{3,1},{4,6},{5,7},{6,4},{7,5},{8,10},{9,11},{10,... | collective-permute-start | bytes 589832 | tf_op jit(solution)/shard_map/ppermute | solution.py:27
  11.4 9.9 %collective-permute-start.3 = (bf16[128,768]{1,0:T(8,128)(2,1)S(1)}, bf16[128,768]{1,0:T(8,128)(2,1)S(1)}, u32[]{:S(2)}, u32[]{:S(2)}) collective-permute-start(bf16[128,768]{1,0:T(8,128)(2,1)S(1)} %get-tuple-element.104.x0.hidden), channel_id=1, source_target_pairs={{0,1},{1,0},{2,3},{3,2},{4,5},{5,4},{6,7},{7,6},{8,9},{9,8},{10,11... | collective-permute-start | bytes 589832 | tf_op jit(solution)/shard_map/ppermute | solution.py:27
  33.6 7.2 %collective-permute-start.8 = (bf16[128,768]{1,0:T(8,128)(2,1)S(1)}, bf16[128,768]{1,0:T(8,128)(2,1)S(1)}, u32[]{:S(2)}, u32[]{:S(2)}) collective-permute-start(bf16[128,768]{1,0:T(8,128)(2,1)S(1)} %get-tuple-element.95), channel_id=1, source_target_pairs={{0,2},{1,3},{2,0},{3,1},{4,6},{5,7},{6,4},{7,5},{8,10},{9,11},{10,... | collective-permute-start | bytes 589832 | tf_op jit(solution)/shard_map/ppermute | solution.py:27
  41.1 8.2 %collective-permute-start.9 = (bf16[128,768]{1,0:T(8,128)(2,1)S(1)}, bf16[128,768]{1,0:T(8,128)(2,1)S(1)}, u32[]{:S(2)}, u32[]{:S(2)}) collective-permute-start(bf16[128,768]{1,0:T(8,128)(2,1)S(1)} %get-tuple-element.53), channel_id=1, source_target_pairs={{0,4},{4,8},{8,12},{12,0},{1,5},{5,9},{9,13},{13,1},{2,6},{6,10},{... | collective-permute-start | bytes 589832 | tf_op jit(solution)/shard_map/ppermute | solution.py:23
  42.8 7.0 %collective-permute-start.13 = (bf16[128,768]{1,0:T(8,128)(2,1)S(1)}, bf16[128,768]{1,0:T(8,128)(2,1)S(1)}, u32[]{:S(2)}, u32[]{:S(2)}) collective-permute-start(bf16[128,768]{1,0:T(8,128)(2,1)S(1)} %get-tuple-element.94), channel_id=1, source_target_pairs={{0,2},{1,3},{2,0},{3,1},{4,6},{5,7},{6,4},{7,5},{8,10},{9,11},{10,... | collective-permute-start | bytes 589832 | tf_op jit(solution)/shard_map/ppermute | solution.py:27
  49.3 5.7 %collective-permute-start.11 = (bf16[128,768]{1,0:T(8,128)(2,1)S(1)}, bf16[128,768]{1,0:T(8,128)(2,1)S(1)}, u32[]{:S(2)}, u32[]{:S(2)}) collective-permute-start(bf16[128,768]{1,0:T(8,128)(2,1)S(1)} %collective-permute-done.9.x0.hidden), channel_id=1, source_target_pairs={{0,2},{1,3},{2,0},{3,1},{4,6},{5,7},{6,4},{7,5},{8,10},{9,11},{10,... | collective-permute-start | bytes 589832 | tf_op jit(solution)/shard_map/ppermute | solution.py:27
  50.1 7.7 %collective-permute-start.14 = (bf16[128,768]{1,0:T(8,128)(2,1)S(1)}, bf16[128,768]{1,0:T(8,128)(2,1)S(1)}, u32[]{:S(2)}, u32[]{:S(2)}) collective-permute-start(bf16[128,768]{1,0:T(8,128)(2,1)S(1)} %get-tuple-element.56), channel_id=1, source_target_pairs={{0,4},{4,8},{8,12},{12,0},{1,5},{5,9},{9,13},{13,1},{2,6},{6,10},{... | collective-permute-start | bytes 589832 | tf_op jit(solution)/shard_map/ppermute | solution.py:23
  51.0 8.4 %collective-permute-start.10 = (bf16[128,768]{1,0:T(8,128)(2,1)S(1)}, bf16[128,768]{1,0:T(8,128)(2,1)S(1)}, u32[]{:S(2)}, u32[]{:S(2)}) collective-permute-start(bf16[128,768]{1,0:T(8,128)(2,1)S(1)} %collective-permute-done.9.x0.hidden), channel_id=1, source_target_pairs={{0,1},{1,0},{2,3},{3,2},{4,5},{5,4},{6,7},{7,6},{8,9},{9,8},{10,11... | collective-permute-start | bytes 589832 | tf_op jit(solution)/shard_map/ppermute | solution.py:27
  57.8 5.7 %collective-permute-start.16 = (bf16[128,768]{1,0:T(8,128)(2,1)S(1)}, bf16[128,768]{1,0:T(8,128)(2,1)S(1)}, u32[]{:S(2)}, u32[]{:S(2)}) collective-permute-start(bf16[128,768]{1,0:T(8,128)(2,1)S(1)} %collective-permute-done.14.x0.hidden), channel_id=1, source_target_pairs={{0,2},{1,3},{2,0},{3,1},{4,6},{5,7},{6,4},{7,5},{8,10},{9,11},{10,... | collective-permute-start | bytes 589832 | tf_op jit(solution)/shard_map/ppermute | solution.py:27
  76.7 7.0 %collective-permute-start.20 = (bf16[128,768]{1,0:T(8,128)(2,1)S(1)}, bf16[128,768]{1,0:T(8,128)(2,1)S(1)}, u32[]{:S(2)}, u32[]{:S(2)}) collective-permute-start(bf16[128,768]{1,0:T(8,128)(2,1)S(1)} %get-tuple-element.93), channel_id=1, source_target_pairs={{0,2},{1,3},{2,0},{3,1},{4,6},{5,7},{6,4},{7,5},{8,10},{9,11},{10,... | collective-permute-start | bytes 589832 | tf_op jit(solution)/shard_map/ppermute | solution.py:27
  84.1 8.7 %collective-permute-start.22 = (bf16[128,768]{1,0:T(8,128)(2,1)S(1)}, bf16[128,768]{1,0:T(8,128)(2,1)S(1)}, u32[]{:S(2)}, u32[]{:S(2)}) collective-permute-start(bf16[128,768]{1,0:T(8,128)(2,1)S(1)} %get-tuple-element.63), channel_id=1, source_target_pairs={{0,4},{4,8},{8,12},{12,0},{1,5},{5,9},{9,13},{13,1},{2,6},{6,10},{... | collective-permute-start | bytes 589832 | tf_op jit(solution)/shard_map/ppermute | solution.py:23
  84.2 9.6 %collective-permute-start.26 = (bf16[128,768]{1,0:T(8,128)(2,1)S(1)}, bf16[128,768]{1,0:T(8,128)(2,1)S(1)}, u32[]{:S(2)}, u32[]{:S(2)}) collective-permute-start(bf16[128,768]{1,0:T(8,128)(2,1)S(1)} %get-tuple-element.92), channel_id=1, source_target_pairs={{0,2},{1,3},{2,0},{3,1},{4,6},{5,7},{6,4},{7,5},{8,10},{9,11},{10,... | collective-permute-start | bytes 589832 | tf_op jit(solution)/shard_map/ppermute | solution.py:27
  92.8 5.8 %collective-permute-start.24 = (bf16[128,768]{1,0:T(8,128)(2,1)S(1)}, bf16[128,768]{1,0:T(8,128)(2,1)S(1)}, u32[]{:S(2)}, u32[]{:S(2)}) collective-permute-start(bf16[128,768]{1,0:T(8,128)(2,1)S(1)} %collective-permute-done.22.x0.hidden), channel_id=1, source_target_pairs={{0,2},{1,3},{2,0},{3,1},{4,6},{5,7},{6,4},{7,5},{8,10},{9,11},{10,... | collective-permute-start | bytes 589832 | tf_op jit(solution)/shard_map/ppermute | solution.py:27
  94.1 7.7 %collective-permute-start.27 = (bf16[128,768]{1,0:T(8,128)(2,1)S(1)}, bf16[128,768]{1,0:T(8,128)(2,1)S(1)}, u32[]{:S(2)}, u32[]{:S(2)}) collective-permute-start(bf16[128,768]{1,0:T(8,128)(2,1)S(1)} %get-tuple-element.66), channel_id=1, source_target_pairs={{0,4},{4,8},{8,12},{12,0},{1,5},{5,9},{9,13},{13,1},{2,6},{6,10},{... | collective-permute-start | bytes 589832 | tf_op jit(solution)/shard_map/ppermute | solution.py:23
  94.7 8.2 %collective-permute-start.23 = (bf16[128,768]{1,0:T(8,128)(2,1)S(1)}, bf16[128,768]{1,0:T(8,128)(2,1)S(1)}, u32[]{:S(2)}, u32[]{:S(2)}) collective-permute-start(bf16[128,768]{1,0:T(8,128)(2,1)S(1)} %collective-permute-done.22.x0.hidden), channel_id=1, source_target_pairs={{0,1},{1,0},{2,3},{3,2},{4,5},{5,4},{6,7},{7,6},{8,9},{9,8},{10,11... | collective-permute-start | bytes 589832 | tf_op jit(solution)/shard_map/ppermute | solution.py:27
  101.9 5.7 %collective-permute-start.29 = (bf16[128,768]{1,0:T(8,128)(2,1)S(1)}, bf16[128,768]{1,0:T(8,128)(2,1)S(1)}, u32[]{:S(2)}, u32[]{:S(2)}) collective-permute-start(bf16[128,768]{1,0:T(8,128)(2,1)S(1)} %collective-permute-done.27.x0.hidden), channel_id=1, source_target_pairs={{0,2},{1,3},{2,0},{3,1},{4,6},{5,7},{6,4},{7,5},{8,10},{9,11},{10,... | collective-permute-start | bytes 589832 | tf_op jit(solution)/shard_map/ppermute | solution.py:27
  120.7 7.0 %collective-permute-start.33 = (bf16[128,768]{1,0:T(8,128)(2,1)S(1)}, bf16[128,768]{1,0:T(8,128)(2,1)S(1)}, u32[]{:S(2)}, u32[]{:S(2)}) collective-permute-start(bf16[128,768]{1,0:T(8,128)(2,1)S(1)} %get-tuple-element.91), channel_id=1, source_target_pairs={{0,2},{1,3},{2,0},{3,1},{4,6},{5,7},{6,4},{7,5},{8,10},{9,11},{10,... | collective-permute-start | bytes 589832 | tf_op jit(solution)/shard_map/ppermute | solution.py:27
  128.1 9.0 %collective-permute-start.35 = (bf16[128,768]{1,0:T(8,128)(2,1)S(1)}, bf16[128,768]{1,0:T(8,128)(2,1)S(1)}, u32[]{:S(2)}, u32[]{:S(2)}) collective-permute-start(bf16[128,768]{1,0:T(8,128)(2,1)S(1)} %get-tuple-element.73), channel_id=1, source_target_pairs={{0,4},{4,8},{8,12},{12,0},{1,5},{5,9},{9,13},{13,1},{2,6},{6,10},{... | collective-permute-start | bytes 589832 | tf_op jit(solution)/shard_map/ppermute | solution.py:23
  129.9 8.2 %collective-permute-start.39 = (bf16[128,768]{1,0:T(8,128)(2,1)S(1)}, bf16[128,768]{1,0:T(8,128)(2,1)S(1)}, u32[]{:S(2)}, u32[]{:S(2)}) collective-permute-start(bf16[128,768]{1,0:T(8,128)(2,1)S(1)} %get-tuple-element.90), channel_id=1, source_target_pairs={{0,2},{1,3},{2,0},{3,1},{4,6},{5,7},{6,4},{7,5},{8,10},{9,11},{10,... | collective-permute-start | bytes 589832 | tf_op jit(solution)/shard_map/ppermute | solution.py:27
  137.1 5.7 %collective-permute-start.37 = (bf16[128,768]{1,0:T(8,128)(2,1)S(1)}, bf16[128,768]{1,0:T(8,128)(2,1)S(1)}, u32[]{:S(2)}, u32[]{:S(2)}) collective-permute-start(bf16[128,768]{1,0:T(8,128)(2,1)S(1)} %collective-permute-done.35.x0.refs_5_), channel_id=1, source_target_pairs={{0,2},{1,3},{2,0},{3,1},{4,6},{5,7},{6,4},{7,5},{8,10},{9,11},{10,... | collective-permute-start | bytes 589832 | tf_op jit(solution)/shard_map/ppermute | solution.py:27
  138.5 7.5 %collective-permute-start.40 = (bf16[128,768]{1,0:T(8,128)(2,1)S(1)}, bf16[128,768]{1,0:T(8,128)(2,1)S(1)}, u32[]{:S(2)}, u32[]{:S(2)}) collective-permute-start(bf16[128,768]{1,0:T(8,128)(2,1)S(1)} %get-tuple-element.76), channel_id=1, source_target_pairs={{0,4},{4,8},{8,12},{12,0},{1,5},{5,9},{9,13},{13,1},{2,6},{6,10},{... | collective-permute-start | bytes 589832 | tf_op jit(solution)/shard_map/ppermute | solution.py:23
  138.6 9.5 %collective-permute-start.36 = (bf16[128,768]{1,0:T(8,128)(2,1)S(1)}, bf16[128,768]{1,0:T(8,128)(2,1)S(1)}, u32[]{:S(2)}, u32[]{:S(2)}) collective-permute-start(bf16[128,768]{1,0:T(8,128)(2,1)S(1)} %collective-permute-done.35.x0.refs_5_), channel_id=1, source_target_pairs={{0,1},{1,0},{2,3},{3,2},{4,5},{5,4},{6,7},{7,6},{8,9},{9,8},{10,11... | collective-permute-start | bytes 589832 | tf_op jit(solution)/shard_map/ppermute | solution.py:27
  146.0 5.7 %collective-permute-start.42 = (bf16[128,768]{1,0:T(8,128)(2,1)S(1)}, bf16[128,768]{1,0:T(8,128)(2,1)S(1)}, u32[]{:S(2)}, u32[]{:S(2)}) collective-permute-start(bf16[128,768]{1,0:T(8,128)(2,1)S(1)} %collective-permute-done.40.x0.refs_5_), channel_id=1, source_target_pairs={{0,2},{1,3},{2,0},{3,1},{4,6},{5,7},{6,4},{7,5},{8,10},{9,11},{10,... | collective-permute-start | bytes 589832 | tf_op jit(solution)/shard_map/ppermute | solution.py:27
  147.1 9.3 %collective-permute-start.44 = (bf16[256,768]{1,0:T(8,128)(2,1)S(1)}, bf16[256,768]{1,0:T(8,128)(2,1)S(1)}, u32[]{:S(2)}, u32[]{:S(2)}) collective-permute-start(bf16[256,768]{1,0:T(8,128)(2,1)S(1)} %pad_maximum_fusion), channel_id=1, source_target_pairs={{12,8},{13,9},{14,10},{15,11},{28,24},{29,25},{30,26},{31,27}} | collective-permute-start | bytes 1179656 | tf_op jit(solution)/shard_map/ppermute | solution.py:357
  164.3 7.8 %collective-permute-start.49 = (bf16[128,768]{1,0:T(8,128)(2,1)S(1)}, bf16[128,768]{1,0:T(8,128)(2,1)S(1)}, u32[]{:S(2)}, u32[]{:S(2)}) collective-permute-start(bf16[128,768]{1,0:T(8,128)(2,1)S(1)} %get-tuple-element.88), channel_id=1, source_target_pairs={{0,2},{1,3},{2,0},{3,1},{4,6},{5,7},{6,4},{7,5},{8,10},{9,11},{10,... | collective-permute-start | bytes 589832 | tf_op jit(solution)/shard_map/ppermute | solution.py:27
  165.3 10.2 %collective-permute-start.47 = (bf16[128,768]{1,0:T(8,128)(2,1)S(1)}, bf16[128,768]{1,0:T(8,128)(2,1)S(1)}, u32[]{:S(2)}, u32[]{:S(2)}) collective-permute-start(bf16[128,768]{1,0:T(8,128)(2,1)S(1)} %get-tuple-element.89), channel_id=1, source_target_pairs={{0,2},{1,3},{2,0},{3,1},{4,6},{5,7},{6,4},{7,5},{8,10},{9,11},{10,... | collective-permute-start | bytes 589832 | tf_op jit(solution)/shard_map/ppermute | solution.py:27
  166.5 9.3 %collective-permute-start.51 = (bf16[256,768]{1,0:T(8,128)(2,1)S(1)}, bf16[256,768]{1,0:T(8,128)(2,1)S(1)}, u32[]{:S(2)}, u32[]{:S(2)}) collective-permute-start(bf16[256,768]{1,0:T(8,128)(2,1)S(1)} %pad_maximum_fusion.1), channel_id=1, source_target_pairs={{12,4},{13,5},{14,6},{15,7},{28,20},{29,21},{30,22},{31,23}} | collective-permute-start | bytes 1179656 | tf_op jit(solution)/shard_map/ppermute | solution.py:357
  172.3 12.2 %collective-permute-start.50 = (bf16[128,768]{1,0:T(8,128)(2,1)S(1)}, bf16[128,768]{1,0:T(8,128)(2,1)S(1)}, u32[]{:S(2)}, u32[]{:S(2)}) collective-permute-start(bf16[128,768]{1,0:T(8,128)(2,1)S(1)} %update.15), channel_id=1, source_target_pairs={{0,4},{4,8},{8,12},{12,0},{1,5},{5,9},{9,13},{13,1},{2,6},{6,10},{... | collective-permute-start | bytes 589832 | tf_op jit(solution)/shard_map/ppermute | solution.py:23
  175.7 12.2 %collective-permute-start.48 = (bf16[128,768]{1,0:T(8,128)(2,1)S(1)}, bf16[128,768]{1,0:T(8,128)(2,1)S(1)}, u32[]{:S(2)}, u32[]{:S(2)}) collective-permute-start(bf16[128,768]{1,0:T(8,128)(2,1)S(1)} %update.14), channel_id=1, source_target_pairs={{0,4},{4,8},{8,12},{12,0},{1,5},{5,9},{9,13},{13,1},{2,6},{6,10},{... | collective-permute-start | bytes 589832 | tf_op jit(solution)/shard_map/ppermute | solution.py:23
  (30 other events, 106.4 us)
where the time goes:
time: 189 us
  waiting for transfers between devices  91.7 us (49%)
  Pallas kernels  58.7 us (31%)
  starting transfers between devices  30.8 us (16%)
  local copies, waits for them, and re-layouts  6.42 us (3%)
    ppermute x40, waiting for transfers between devices, swapped(): lax.ppermute(value, axis, [(i, i ^ bit) for i in range(lax.axis_size(axis...  51.1 us
    ppermute x8, waiting for transfers between devices, shifted(): return lax.ppermute(value, axis, pairs)  40.6 us
    pallas_call x8, Pallas kernels, project(): pl.pallas_call(functools.partial(project_kernel, width, tick), out_shape=...  25.5 us
    ppermute x40, starting transfers between devices, swapped(): lax.ppermute(value, axis, [(i, i ^ bit) for i in range(lax.axis_size(axis...  22.7 us
    pallas_call x4, Pallas kernels, attend(): pl.pallas_call(functools.partial(attend_kernel, tick, len(fresh), len(arr...  22.3 us
    pallas_call x4, Pallas kernels, output(): pl.pallas_call(output_kernel, out_shape=jax.ShapeDtypeStruct((3,) + heads...  5.99 us
    unnamed x20, local copies, waits for them, and re-layouts  5.15 us
    ppermute x8, starting transfers between devices, shifted(): return lax.ppermute(value, axis, pairs)  5.1 us
  transfers between devices with their start and end apart: 52, of which 26 were waited for; matrix products, arithmetic and copies ran while one was open for 0% of the time, Pallas kernels for 13%

commit v1 on v0

--- a/solution.py
+++ b/solution.py
@@ -11,6 +11,7 @@
 HEAD_DIM = 64
 LANES = 128
 CHUNKS = 2
+LAST_CHUNKS = 4
 VMEM_BYTES = 12 << 20
 
 IN_VMEM = pl.BlockSpec(memory_space=pltpu.VMEM)
@@ -54,7 +55,7 @@
         in_specs=[pl.BlockSpec(memory_space=pltpu.HBM)],
         out_specs=IN_VMEM,
         scratch_shapes=[pltpu.SemaphoreType.DMA],
-        compiler_params=pltpu.CompilerParams(vmem_limit_bytes=VMEM_BYTES),
+        compiler_params=pltpu.CompilerParams(vmem_limit_bytes=38 << 20),
         cost_estimate=pl.CostEstimate(flops=0, bytes_accessed=4 * weight.size, transcendentals=0),
         name="preload",
     )(weight)
@@ -232,10 +233,22 @@
 
 
 def update_kernel(
-    tick, start, step_ids, step_sizes, own, side, arrived, hidden, latent, mods, sent, advanced
+    tick,
+    start,
+    offset,
+    step_ids,
+    step_sizes,
+    own,
+    side,
+    arrived,
+    hidden,
+    latent,
+    mods,
+    sent,
+    advanced,
 ):
     me, segment = position("head"), position("segment")
-    rows, width = hidden.shape
+    rows, width = arrived.shape
     step = whole(step_ids[tick : tick + 1, :], segment)
     cut = pl.ds(start, rows)
     attended = (
@@ -245,30 +258,31 @@
     )
     at = pl.multiple_of(me * width, width)
     gate = 1.0 + mods[2, pl.ds(step, 1), pl.ds(at, width)]
-    updated = (hidden[...].astype(jnp.float32) + gate * attended).astype(jnp.bfloat16)
+    before = hidden[pl.ds(offset, rows), :].astype(jnp.float32)
+    updated = (before + gate * attended).astype(jnp.bfloat16)
     sent[...] = updated
     if advanced is not None:
-        moved = (
-            latent[cut, :].astype(jnp.float32) + entry(step_sizes[...], step) * updated.astype(jnp.float32)
-        ).astype(jnp.bfloat16)
-        advanced[...] = moved
         is_last = segment == lax.axis_size("segment") - 1
 
         @pl.when(is_last)
         def _():
+            moved = (
+                latent[cut, :].astype(jnp.float32) + entry(step_sizes[...], step) * updated.astype(jnp.float32)
+            ).astype(jnp.bfloat16)
+            advanced[...] = moved
             sent[...] = moved
 
 
-def update(tick, start, tables, own, side, arrived, hidden, latent, mods):
-    out = jax.ShapeDtypeStruct(hidden.shape, hidden.dtype)
+def update(tick, start, offset, tables, own, side, arrived, hidden, latent, mods):
+    out = jax.ShapeDtypeStruct(arrived.shape, arrived.dtype)
     if latent is None:
 
         def body(*refs):
-            update_kernel(tick, start, *refs[:6], None, *refs[6:8], None)
+            update_kernel(tick, start, offset, *refs[:6], None, *refs[6:8], None)
 
         arrays, outs = (own, side, arrived, hidden, mods), 1
     else:
-        body = functools.partial(update_kernel, tick, start)
+        body = functools.partial(update_kernel, tick, start, offset)
         arrays, outs = (own, side, arrived, hidden, latent, mods), 2
     return pl.pallas_call(
         body,
@@ -277,21 +291,23 @@
         out_specs=(IN_VMEM,) * outs,
         compiler_params=pltpu.CompilerParams(vmem_limit_bytes=VMEM_BYTES),
         cost_estimate=pl.CostEstimate(
-            flops=8 * hidden.size, bytes_accessed=16 * hidden.size, transcendentals=0
+            flops=8 * arrived.size, bytes_accessed=16 * arrived.size, transcendentals=0
         ),
         name="update",
     )(*tables, *arrays)
 
 
-def finish_kernel(cuts, count, step_ids, step_sizes, latent, *refs):
+def finish_kernel(cuts, kept_cuts, count, step_ids, step_sizes, latent, *refs):
     segment = position("segment")
     last = lax.axis_size("segment") - 1
     parts = refs[: len(cuts)]
-    kept = refs[len(cuts) : 2 * len(cuts)]
-    moved = refs[2 * len(cuts) : 2 * len(cuts) + count]
-    out_hidden, out_latent = refs[2 * len(cuts) + count :]
-    for cut, part, piece in zip(cuts, parts, kept):
+    both = len(cuts) + len(kept_cuts)
+    kept = refs[len(cuts) : both]
+    moved = refs[both : both + count]
+    out_hidden, out_latent = refs[both + count :]
+    for cut, part in zip(cuts, parts):
         out_hidden[cut, :] = part[...]
+    for cut, piece in zip(kept_cuts, kept):
         out_latent[cut, :] = piece[...]
     for k, array in enumerate(moved):
 
@@ -310,11 +326,11 @@
             out_latent[cut, :] = advanced
 
 
-def finish(cuts, tables, latent, parts, kept, moved):
+def finish(cuts, kept_cuts, tables, latent, parts, kept, moved):
     out = jax.ShapeDtypeStruct(latent.shape, latent.dtype)
     arrays = (latent, *parts, *kept, *moved)
     return pl.pallas_call(
-        functools.partial(finish_kernel, cuts, len(moved)),
+        functools.partial(finish_kernel, cuts, kept_cuts, len(moved)),
         out_shape=(out, out),
         in_specs=[IN_VMEM] * (2 + len(arrays)),
         out_specs=(IN_VMEM, IN_VMEM),
@@ -375,19 +391,22 @@
         far_in = swapped(far, "head", 1)
         own, side, near = output(heads, projection)
         side_in = swapped(side, "head", 1)
+        count = CHUNKS if k < ticks - 1 else LAST_CHUNKS
+        pieces = [slice(c * rows // count, (c + 1) * rows // count) for c in range(count)]
         sums = [
             (near[cut].astype(jnp.float32) + far_in[cut].astype(jnp.float32)).astype(jnp.bfloat16)
-            for cut in cuts
+            for cut in pieces
         ]
         crossed = []
-        for c in range(CHUNKS):
+        for c in range(count):
             crossed.append(swapped(sums[c], "head", 2))
         advanced_parts = []
         sent = []
-        for c, part in enumerate(hidden):
+        for c, cut in enumerate(pieces):
             latent = latents[k] if k < last else None
+            part, offset = hidden[cut.start // step_rows], cut.start % step_rows
             onward, *advanced = update(
-                k, cuts[c].start, steps, own, side_in, crossed[c], part, latent, mods
+                k, cut.start, offset, steps, own, side_in, crossed[c], part, latent, mods
             )
             advanced_parts += advanced
             sent.append(shifted(onward, "segment", 1))
@@ -396,7 +415,7 @@
             kept = advanced_parts
         elif k < last:
             done = jnp.concatenate(advanced_parts, axis=0)
-    return finish(cuts, steps, latent_in, hidden, kept, moved)
+    return finish(pieces, cuts, steps, latent_in, hidden, kept, moved)
 
 
 def normalize(hidden_rows, shift_vec, scale_vec):
@@ -496,7 +515,7 @@
         fits = (
             shape["head"] == 4
             and hidden_in.shape[1] % LANES == 0
-            and hidden_in.shape[0] % (16 * CHUNKS) == 0
+            and hidden_in.shape[0] % (16 * LAST_CHUNKS) == 0
             and ticks == shape["segment"]
             and ticks > 1
         )

time: 189 us -> 186 us (0.984)
  local copies, waits for them, and re-layouts: 6.42 us -> 1.31 us
  waiting for transfers between devices: 91.7 us -> 87.6 us
  starting transfers between devices: 30.8 us -> 34 us
  Pallas kernels: 58.7 us -> 61.8 us
    unnamed x20 -> x18, local copies, waits for them, and re-layouts: 5.15 us -> 0.05 us
    pallas_call x1, Pallas kernels: 0.95 us -> 5.09 us  [preload(): pl.pallas_call(preload_kernel, out_shape=pltpu.VMEM(weight.shape, weight....]
    ppermute x8 -> x10, waiting for transfers between devices: 40.6 us -> 37.2 us  [shifted(): return lax.ppermute(value, axis, pairs)]
    ppermute x40 -> x42, starting transfers between devices: 22.7 us -> 24.6 us  [swapped(): lax.ppermute(value, axis, [(i, i ^ bit) for i in range(lax.axis_size(axis...]
    ppermute x8 -> x10, starting transfers between devices: 5.1 us -> 6.43 us  [shifted(): return lax.ppermute(value, axis, pairs)]
    ppermute x40 -> x42, waiting for transfers between devices: 51.1 us -> 50.4 us  [swapped(): lax.ppermute(value, axis, [(i, i ^ bit) for i in range(lax.axis_size(axis...]
  transfers between devices with their start and end apart: 52 -> 56, of which waited for: 26 -> 31; matrix products, arithmetic and copies ran while one was open for 0% -> 0% of each run, Pallas kernels for 13% -> 14%
where the time goes in v1:
time: 186 us
  waiting for transfers between devices  87.6 us (47%)
  Pallas kernels  61.8 us (33%)
  starting transfers between devices  34 us (18%)
    ppermute x42, waiting for transfers between devices, swapped(): lax.ppermute(value, axis, [(i, i ^ bit) for i in range(lax.axis_size(axis...  50.4 us
    ppermute x10, waiting for transfers between devices, shifted(): return lax.ppermute(value, axis, pairs)  37.2 us
    pallas_call x8, Pallas kernels, project(): pl.pallas_call(functools.partial(project_kernel, width, tick), out_shape=...  24.9 us
    ppermute x42, starting transfers between devices, swapped(): lax.ppermute(value, axis, [(i, i ^ bit) for i in range(lax.axis_size(axis...  24.6 us
    pallas_call x4, Pallas kernels, attend(): pl.pallas_call(functools.partial(attend_kernel, tick, len(fresh), len(arr...  22.3 us
    ppermute x10, starting transfers between devices, shifted(): return lax.ppermute(value, axis, pairs)  6.43 us
    pallas_call x4, Pallas kernels, output(): pl.pallas_call(output_kernel, out_shape=jax.ShapeDtypeStruct((3,) + heads...  6.01 us
    pallas_call x1, Pallas kernels, preload(): pl.pallas_call(preload_kernel, out_shape=pltpu.VMEM(weight.shape, weight....  5.09 us
  transfers between devices with their start and end apart: 56, of which 31 were waited for; matrix products, arithmetic and copies ran while one was open for 0% of the time, Pallas kernels for 14%

profile of v1, /device:TPU:0, one launch (start us, length us, event | category | flops | bytes accessed | tf_op | source)
XLA Modules:
  0.0 186.3 jit_solution(4286019983328743220)
XLA Ops:
  1.7 3.1 %collective-permute-start.1 = (bf16[128,768]{1,0:T(8,128)(2,1)S(1)}, bf16[128,768]{1,0:T(8,128)(2,1)S(1)}, u32[]{:S(2)}, u32[]{:S(2)}) collective-permute-start(bf16[128,768]{1,0:T(8,128)(2,1)S(1)} %get-tuple-element.107.x0.hidden), channel_id=1, source_target_pairs={{0,2},{1,3},{2,0},{3,1},{4,6},{5,7},{6,4},{7,5},{8,10},{9,11},{10,... | collective-permute-start | bytes 589832 | tf_op jit(solution)/shard_map/ppermute | solution.py:28
  4.7 4.9 %collective-permute-done.1.x2 = bf16[128,768]{1,0:T(8,128)(2,1)S(1)} collective-permute-done((bf16[128,768]{1,0:T(8,128)(2,1)S(1)}, bf16[128,768]{1,0:T(8,128)(2,1)S(1)}, u32[]{:S(2)}, u32[]{:S(2)}) %collective-permute-start.1) | collective-permute-done | bytes 196640 | tf_op jit(solution)/shard_map/ppermute | solution.py:28
  11.6 5.1 %preload.1.weight = bf16[3,3072,768]{2,1,0:T(8,128)(2,1)S(1)} custom-call(bf16[3,3072,768]{2,1,0:T(8,128)(2,1)} %bitcast.120), custom_call_target="tpu_custom_call" | custom-call | bytes 28311552 | tf_op jit(solution)/shard_map/preload/pallas_call | solution.py:52
  16.8 3.1 %project.8 = (bf16[128,768]{1,0:T(8,128)(2,1)S(1)}, bf16[2,128,768]{2,1,0:T(8,128)(2,1)S(1)}) custom-call(s32[4,4]{1,0:T(4,128)S(1)} %copy-done.2, bf16[128,768]{1,0:T(8,128)(2,1)S(1)} %get-tuple-element.107.x0.hidden, bf16[128,768]{1,0:T(8,128)(2,1)S(1)} %collective-permute-done.x1, bf16[128,768]{1,0:T(8,128)(2,1)S(1)} %collective-permute-done.1.x2, ...), custom_call_target="tpu_custom_call" | custom-call | flops 1811939328 | bytes 1376256 | tf_op jit(solution)/shard_map/project/pallas_call | solution.py:100
  21.5 3.1 %project.9 = (bf16[128,768]{1,0:T(8,128)(2,1)S(1)}, bf16[2,128,768]{2,1,0:T(8,128)(2,1)S(1)}) custom-call(s32[4,4]{1,0:T(4,128)S(1)} %copy-done.2, bf16[128,768]{1,0:T(8,128)(2,1)S(1)} %get-tuple-element.106.x0.hidden, bf16[128,768]{1,0:T(8,128)(2,1)S(1)} %collective-permute-done.3.x1, bf16[128,768]{1,0:T(8,128)(2,1)S(1)} %collective-permute-done.4.x2, ...), custom_call_target="tpu_custom_call" | custom-call | flops 1811939328 | bytes 1376256 | tf_op jit(solution)/shard_map/project/pallas_call | solution.py:100
  24.7 5.6 %attend.4 = (bf16[256,768]{1,0:T(8,128)(2,1)S(1)}, bf16[256,768]{1,0:T(8,128)(2,1)S(1)}, bf16[2,1024,768]{2,1,0:T(8,128)(2,1)S(1)}) custom-call(s32[4,4]{1,0:T(4,128)S(1)} %copy-done.5, s32[1,4]{1,0:T(1,128)S(1)} %bitcast.116, bf16[2,1024,768]{2,1,0:T(8,128)(2,1)S(1)} %bitcast.115, bf16[768,3072]{1,0:T(8,128)(2,1)S(1)} %bitcast.96, ...), custom_call_target="tpu_custom_call" | custom-call | flops 3825205248 | bytes 2752512 | tf_op jit(solution)/shard_map/attend/pallas_call | solution.py:192
  33.9 5.8 %collective-permute-done.8.arrived = bf16[128,768]{1,0:T(8,128)(2,1)S(1)} collective-permute-done((bf16[128,768]{1,0:T(8,128)(2,1)S(1)}, bf16[128,768]{1,0:T(8,128)(2,1)S(1)}, u32[]{:S(2)}, u32[]{:S(2)}) %collective-permute-start.8) | collective-permute-done | bytes 196640 | tf_op jit(solution)/shard_map/ppermute | solution.py:28
  42.1 6.2 %collective-permute-done.9.x0.hidden = bf16[128,768]{1,0:T(8,128)(2,1)S(1)} collective-permute-done((bf16[128,768]{1,0:T(8,128)(2,1)S(1)}, bf16[128,768]{1,0:T(8,128)(2,1)S(1)}, u32[]{:S(2)}, u32[]{:S(2)}) %collective-permute-start.9) | collective-permute-done | bytes 196640 | tf_op jit(solution)/shard_map/ppermute | solution.py:24
  49.8 4.2 %collective-permute-done.11.x2 = bf16[128,768]{1,0:T(8,128)(2,1)S(1)} collective-permute-done((bf16[128,768]{1,0:T(8,128)(2,1)S(1)}, bf16[128,768]{1,0:T(8,128)(2,1)S(1)}, u32[]{:S(2)}, u32[]{:S(2)}) %collective-permute-start.11) | collective-permute-done | bytes 196640 | tf_op jit(solution)/shard_map/ppermute | solution.py:28
  54.0 2.7 %collective-permute-done.14.x0.hidden = bf16[128,768]{1,0:T(8,128)(2,1)S(1)} collective-permute-done((bf16[128,768]{1,0:T(8,128)(2,1)S(1)}, bf16[128,768]{1,0:T(8,128)(2,1)S(1)}, u32[]{:S(2)}, u32[]{:S(2)}) %collective-permute-start.14) | collective-permute-done | bytes 196640 | tf_op jit(solution)/shard_map/ppermute | solution.py:24
  58.3 3.1 %project.10 = (bf16[128,768]{1,0:T(8,128)(2,1)S(1)}, bf16[2,128,768]{2,1,0:T(8,128)(2,1)S(1)}) custom-call(s32[4,4]{1,0:T(4,128)S(1)} %copy-done.2, bf16[128,768]{1,0:T(8,128)(2,1)S(1)} %collective-permute-done.9.x0.hidden, bf16[128,768]{1,0:T(8,128)(2,1)S(1)} %collective-permute-done.10.x1, bf16[128,768]{1,0:T(8,128)(2,1)S(1)} %collective-permute-done.11.x2, ...), custom_call_target="tpu_custom_call" | custom-call | flops 1811939328 | bytes 1376256 | tf_op jit(solution)/shard_map/project/pallas_call | solution.py:100
  63.8 3.1 %project.11 = (bf16[128,768]{1,0:T(8,128)(2,1)S(1)}, bf16[2,128,768]{2,1,0:T(8,128)(2,1)S(1)}) custom-call(s32[4,4]{1,0:T(4,128)S(1)} %copy-done.2, bf16[128,768]{1,0:T(8,128)(2,1)S(1)} %collective-permute-done.14.x0.hidden, bf16[128,768]{1,0:T(8,128)(2,1)S(1)} %collective-permute-done.15.x1, bf16[128,768]{1,0:T(8,128)(2,1)S(1)} %collective-permute-done.16.x2, ...), custom_call_target="tpu_custom_call" | custom-call | flops 1811939328 | bytes 1376256 | tf_op jit(solution)/shard_map/project/pallas_call | solution.py:100
  66.9 5.6 %attend.5 = (bf16[256,768]{1,0:T(8,128)(2,1)S(1)}, bf16[256,768]{1,0:T(8,128)(2,1)S(1)}, bf16[2,1024,768]{2,1,0:T(8,128)(2,1)S(1)}) custom-call(s32[4,4]{1,0:T(4,128)S(1)} %copy-done.5, s32[1,4]{1,0:T(1,128)S(1)} %bitcast.117, bf16[2,1024,768]{2,1,0:T(8,128)(2,1)S(1)} %get-tuple-element.50.refs_2_, bf16[768,3072]{1,0:T(8,128)(2,1)S(1)} %bitcast.98, ...), custom_call_target="tpu_custom_call" | custom-call | flops 3825205248 | bytes 2752512 | tf_op jit(solution)/shard_map/attend/pallas_call | solution.py:192
  77.2 5.3 %collective-permute-done.20.arrived = bf16[128,768]{1,0:T(8,128)(2,1)S(1)} collective-permute-done((bf16[128,768]{1,0:T(8,128)(2,1)S(1)}, bf16[128,768]{1,0:T(8,128)(2,1)S(1)}, u32[]{:S(2)}, u32[]{:S(2)}) %collective-permute-start.20) | collective-permute-done | bytes 196640 | tf_op jit(solution)/shard_map/ppermute | solution.py:28
  84.5 7.3 %collective-permute-done.22.x0.hidden = bf16[128,768]{1,0:T(8,128)(2,1)S(1)} collective-permute-done((bf16[128,768]{1,0:T(8,128)(2,1)S(1)}, bf16[128,768]{1,0:T(8,128)(2,1)S(1)}, u32[]{:S(2)}, u32[]{:S(2)}) %collective-permute-start.22) | collective-permute-done | bytes 196640 | tf_op jit(solution)/shard_map/ppermute | solution.py:24
  93.5 4.0 %collective-permute-done.24.x2 = bf16[128,768]{1,0:T(8,128)(2,1)S(1)} collective-permute-done((bf16[128,768]{1,0:T(8,128)(2,1)S(1)}, bf16[128,768]{1,0:T(8,128)(2,1)S(1)}, u32[]{:S(2)}, u32[]{:S(2)}) %collective-permute-start.24) | collective-permute-done | bytes 196640 | tf_op jit(solution)/shard_map/ppermute | solution.py:28
  97.5 3.3 %collective-permute-done.27.x0.hidden = bf16[128,768]{1,0:T(8,128)(2,1)S(1)} collective-permute-done((bf16[128,768]{1,0:T(8,128)(2,1)S(1)}, bf16[128,768]{1,0:T(8,128)(2,1)S(1)}, u32[]{:S(2)}, u32[]{:S(2)}) %collective-permute-start.27) | collective-permute-done | bytes 196640 | tf_op jit(solution)/shard_map/ppermute | solution.py:24
  101.8 3.1 %project.12 = (bf16[128,768]{1,0:T(8,128)(2,1)S(1)}, bf16[2,128,768]{2,1,0:T(8,128)(2,1)S(1)}) custom-call(s32[4,4]{1,0:T(4,128)S(1)} %copy-done.2, bf16[128,768]{1,0:T(8,128)(2,1)S(1)} %collective-permute-done.22.x0.hidden, bf16[128,768]{1,0:T(8,128)(2,1)S(1)} %collective-permute-done.23.x1, bf16[128,768]{1,0:T(8,128)(2,1)S(1)} %collective-permute-done.24.x2, ...), custom_call_target="tpu_custom_call" | custom-call | flops 1811939328 | bytes 1376256 | tf_op jit(solution)/shard_map/project/pallas_call | solution.py:100
  108.0 3.1 %project.13 = (bf16[128,768]{1,0:T(8,128)(2,1)S(1)}, bf16[2,128,768]{2,1,0:T(8,128)(2,1)S(1)}) custom-call(s32[4,4]{1,0:T(4,128)S(1)} %copy-done.2, bf16[128,768]{1,0:T(8,128)(2,1)S(1)} %collective-permute-done.27.x0.hidden, bf16[128,768]{1,0:T(8,128)(2,1)S(1)} %collective-permute-done.28.x1, bf16[128,768]{1,0:T(8,128)(2,1)S(1)} %collective-permute-done.29.x2, ...), custom_call_target="tpu_custom_call" | custom-call | flops 1811939328 | bytes 1376256 | tf_op jit(solution)/shard_map/project/pallas_call | solution.py:100
  111.1 5.5 %attend.6 = (bf16[256,768]{1,0:T(8,128)(2,1)S(1)}, bf16[256,768]{1,0:T(8,128)(2,1)S(1)}, bf16[2,1024,768]{2,1,0:T(8,128)(2,1)S(1)}) custom-call(s32[4,4]{1,0:T(4,128)S(1)} %copy-done.5, s32[1,4]{1,0:T(1,128)S(1)} %bitcast.118, bf16[2,1024,768]{2,1,0:T(8,128)(2,1)S(1)} %get-tuple-element.60.refs_2_, bf16[768,3072]{1,0:T(8,128)(2,1)S(1)} %bitcast.100, ...), custom_call_target="tpu_custom_call" | custom-call | flops 3825205248 | bytes 2752512 | tf_op jit(solution)/shard_map/attend/pallas_call | solution.py:192
  120.9 5.8 %collective-permute-done.33.arrived = bf16[128,768]{1,0:T(8,128)(2,1)S(1)} collective-permute-done((bf16[128,768]{1,0:T(8,128)(2,1)S(1)}, bf16[128,768]{1,0:T(8,128)(2,1)S(1)}, u32[]{:S(2)}, u32[]{:S(2)}) %collective-permute-start.33) | collective-permute-done | bytes 196640 | tf_op jit(solution)/shard_map/ppermute | solution.py:28
  126.9 2.0 %collective-permute-start.35 = (bf16[128,768]{1,0:T(8,128)(2,1)S(1)}, bf16[128,768]{1,0:T(8,128)(2,1)S(1)}, u32[]{:S(2)}, u32[]{:S(2)}) collective-permute-start(bf16[128,768]{1,0:T(8,128)(2,1)S(1)} %get-tuple-element.73), channel_id=1, source_target_pairs={{0,4},{4,8},{8,12},{12,0},{1,5},{5,9},{9,13},{13,1},{2,6},{6,10},{... | collective-permute-start | bytes 589832 | tf_op jit(solution)/shard_map/ppermute | solution.py:24
  129.8 6.4 %collective-permute-done.35.x0.refs_5_ = bf16[128,768]{1,0:T(8,128)(2,1)S(1)} collective-permute-done((bf16[128,768]{1,0:T(8,128)(2,1)S(1)}, bf16[128,768]{1,0:T(8,128)(2,1)S(1)}, u32[]{:S(2)}, u32[]{:S(2)}) %collective-permute-start.35) | collective-permute-done | bytes 196640 | tf_op jit(solution)/shard_map/ppermute | solution.py:24
  137.6 4.4 %collective-permute-done.37.x2 = bf16[128,768]{1,0:T(8,128)(2,1)S(1)} collective-permute-done((bf16[128,768]{1,0:T(8,128)(2,1)S(1)}, bf16[128,768]{1,0:T(8,128)(2,1)S(1)}, u32[]{:S(2)}, u32[]{:S(2)}) %collective-permute-start.37) | collective-permute-done | bytes 196640 | tf_op jit(solution)/shard_map/ppermute | solution.py:28
  142.0 3.0 %collective-permute-done.40.x0.refs_5_ = bf16[128,768]{1,0:T(8,128)(2,1)S(1)} collective-permute-done((bf16[128,768]{1,0:T(8,128)(2,1)S(1)}, bf16[128,768]{1,0:T(8,128)(2,1)S(1)}, u32[]{:S(2)}, u32[]{:S(2)}) %collective-permute-start.40) | collective-permute-done | bytes 196640 | tf_op jit(solution)/shard_map/ppermute | solution.py:24
  147.2 3.1 %project.14 = (bf16[128,768]{1,0:T(8,128)(2,1)S(1)}, bf16[2,128,768]{2,1,0:T(8,128)(2,1)S(1)}) custom-call(s32[4,4]{1,0:T(4,128)S(1)} %copy-done.2, bf16[128,768]{1,0:T(8,128)(2,1)S(1)} %collective-permute-done.35.x0.refs_5_, bf16[128,768]{1,0:T(8,128)(2,1)S(1)} %collective-permute-done.36.x1, bf16[128,768]{1,0:T(8,128)(2,1)S(1)} %collective-permute-done.37.x2, ...), custom_call_target="tpu_custom_call" | custom-call | flops 1811939328 | bytes 1376256 | tf_op jit(solution)/shard_map/project/pallas_call | solution.py:100
  152.1 3.1 %project.15 = (bf16[128,768]{1,0:T(8,128)(2,1)S(1)}, bf16[2,128,768]{2,1,0:T(8,128)(2,1)S(1)}) custom-call(s32[4,4]{1,0:T(4,128)S(1)} %copy-done.2, bf16[128,768]{1,0:T(8,128)(2,1)S(1)} %collective-permute-done.40.x0.refs_5_, bf16[128,768]{1,0:T(8,128)(2,1)S(1)} %collective-permute-done.41.x1, bf16[128,768]{1,0:T(8,128)(2,1)S(1)} %collective-permute-done.42.x2, ...), custom_call_target="tpu_custom_call" | custom-call | flops 1811939328 | bytes 1376256 | tf_op jit(solution)/shard_map/project/pallas_call | solution.py:100
  155.3 5.6 %attend.7 = (bf16[256,768]{1,0:T(8,128)(2,1)S(1)}, bf16[256,768]{1,0:T(8,128)(2,1)S(1)}) custom-call(s32[4,4]{1,0:T(4,128)S(1)} %copy-done.5, s32[1,4]{1,0:T(1,128)S(1)} %bitcast.119, bf16[2,1024,768]{2,1,0:T(8,128)(2,1)S(1)} %get-tuple-element.70.refs_2_, bf16[768,3072]{1,0:T(8,128)(2,1)S(1)} %bitcast.102, bf16[128,768]{1,0:T(8,128)(2,1)S(1)} %get-tuple-element.74.refs_4_, ...), custom_call_target="tpu_custom_call" | custom-call | flops 3825205248 | bytes 2752512 | tf_op jit(solution)/shard_map/attend/pallas_call | solution.py:192
  170.2 1.9 %collective-permute-done.51.refs_4_ = bf16[64,768]{1,0:T(8,128)(2,1)S(1)} collective-permute-done((bf16[64,768]{1,0:T(8,128)(2,1)S(1)}, bf16[64,768]{1,0:T(8,128)(2,1)S(1)}, u32[]{:S(2)}, u32[]{:S(2)}) %collective-permute-start.51) | collective-permute-done | bytes 98336 | tf_op jit(solution)/shard_map/ppermute | solution.py:28
  176.8 2.3 %collective-permute-done.54.refs_3_ = bf16[64,768]{1,0:T(8,128)(2,1)S(1)} collective-permute-done((bf16[64,768]{1,0:T(8,128)(2,1)S(1)}, bf16[64,768]{1,0:T(8,128)(2,1)S(1)}, u32[]{:S(2)}, u32[]{:S(2)}) %collective-permute-start.54) | collective-permute-done | bytes 98336 | tf_op jit(solution)/shard_map/ppermute | solution.py:24
  179.0 2.1 %collective-permute-done.52.refs_2_ = bf16[64,768]{1,0:T(8,128)(2,1)S(1)} collective-permute-done((bf16[64,768]{1,0:T(8,128)(2,1)S(1)}, bf16[64,768]{1,0:T(8,128)(2,1)S(1)}, u32[]{:S(2)}, u32[]{:S(2)}) %collective-permute-start.52) | collective-permute-done | bytes 98336 | tf_op jit(solution)/shard_map/ppermute | solution.py:24
  181.2 2.1 %collective-permute-done.50.refs_1_ = bf16[64,768]{1,0:T(8,128)(2,1)S(1)} collective-permute-done((bf16[64,768]{1,0:T(8,128)(2,1)S(1)}, bf16[64,768]{1,0:T(8,128)(2,1)S(1)}, u32[]{:S(2)}, u32[]{:S(2)}) %collective-permute-start.50) | collective-permute-done | bytes 98336 | tf_op jit(solution)/shard_map/ppermute | solution.py:24
  (138 shorter events, 56.0 us)
Async XLA Ops:
  1.7 8.0 %collective-permute-start.1 = (bf16[128,768]{1,0:T(8,128)(2,1)S(1)}, bf16[128,768]{1,0:T(8,128)(2,1)S(1)}, u32[]{:S(2)}, u32[]{:S(2)}) collective-permute-start(bf16[128,768]{1,0:T(8,128)(2,1)S(1)} %get-tuple-element.107.x0.hidden), channel_id=1, source_target_pairs={{0,2},{1,3},{2,0},{3,1},{4,6},{5,7},{6,4},{7,5},{8,10},{9,11},{10,... | collective-permute-start | bytes 589832 | tf_op jit(solution)/shard_map/ppermute | solution.py:28
  4.7 12.0 %collective-permute-start = (bf16[128,768]{1,0:T(8,128)(2,1)S(1)}, bf16[128,768]{1,0:T(8,128)(2,1)S(1)}, u32[]{:S(2)}, u32[]{:S(2)}) collective-permute-start(bf16[128,768]{1,0:T(8,128)(2,1)S(1)} %get-tuple-element.107.x0.hidden), channel_id=1, source_target_pairs={{0,1},{1,0},{2,3},{3,2},{4,5},{5,4},{6,7},{7,6},{8,9},{9,8},{10,11... | collective-permute-start | bytes 589832 | tf_op jit(solution)/shard_map/ppermute | solution.py:28
  9.6 7.1 %collective-permute-start.2 = (bf16[128,768]{1,0:T(8,128)(2,1)S(1)}, bf16[128,768]{1,0:T(8,128)(2,1)S(1)}, u32[]{:S(2)}, u32[]{:S(2)}) collective-permute-start(bf16[128,768]{1,0:T(8,128)(2,1)S(1)} %collective-permute-done.1.x2), channel_id=1, source_target_pairs={{0,1},{1,0},{2,3},{3,2},{4,5},{5,4},{6,7},{7,6},{8,9},{9,8},{10,11... | collective-permute-start | bytes 589832 | tf_op jit(solution)/shard_map/ppermute | solution.py:28
  9.6 10.2 %collective-permute-start.4 = (bf16[128,768]{1,0:T(8,128)(2,1)S(1)}, bf16[128,768]{1,0:T(8,128)(2,1)S(1)}, u32[]{:S(2)}, u32[]{:S(2)}) collective-permute-start(bf16[128,768]{1,0:T(8,128)(2,1)S(1)} %get-tuple-element.106.x0.hidden), channel_id=1, source_target_pairs={{0,2},{1,3},{2,0},{3,1},{4,6},{5,7},{6,4},{7,5},{8,10},{9,11},{10,... | collective-permute-start | bytes 589832 | tf_op jit(solution)/shard_map/ppermute | solution.py:28
  11.4 8.9 %collective-permute-start.3 = (bf16[128,768]{1,0:T(8,128)(2,1)S(1)}, bf16[128,768]{1,0:T(8,128)(2,1)S(1)}, u32[]{:S(2)}, u32[]{:S(2)}) collective-permute-start(bf16[128,768]{1,0:T(8,128)(2,1)S(1)} %get-tuple-element.106.x0.hidden), channel_id=1, source_target_pairs={{0,1},{1,0},{2,3},{3,2},{4,5},{5,4},{6,7},{7,6},{8,9},{9,8},{10,11... | collective-permute-start | bytes 589832 | tf_op jit(solution)/shard_map/ppermute | solution.py:28
  32.6 7.1 %collective-permute-start.8 = (bf16[128,768]{1,0:T(8,128)(2,1)S(1)}, bf16[128,768]{1,0:T(8,128)(2,1)S(1)}, u32[]{:S(2)}, u32[]{:S(2)}) collective-permute-start(bf16[128,768]{1,0:T(8,128)(2,1)S(1)} %get-tuple-element.97), channel_id=1, source_target_pairs={{0,2},{1,3},{2,0},{3,1},{4,6},{5,7},{6,4},{7,5},{8,10},{9,11},{10,... | collective-permute-start | bytes 589832 | tf_op jit(solution)/shard_map/ppermute | solution.py:28
  40.0 8.3 %collective-permute-start.9 = (bf16[128,768]{1,0:T(8,128)(2,1)S(1)}, bf16[128,768]{1,0:T(8,128)(2,1)S(1)}, u32[]{:S(2)}, u32[]{:S(2)}) collective-permute-start(bf16[128,768]{1,0:T(8,128)(2,1)S(1)} %get-tuple-element.53), channel_id=1, source_target_pairs={{0,4},{4,8},{8,12},{12,0},{1,5},{5,9},{9,13},{13,1},{2,6},{6,10},{... | collective-permute-start | bytes 589832 | tf_op jit(solution)/shard_map/ppermute | solution.py:24
  41.6 7.1 %collective-permute-start.13 = (bf16[128,768]{1,0:T(8,128)(2,1)S(1)}, bf16[128,768]{1,0:T(8,128)(2,1)S(1)}, u32[]{:S(2)}, u32[]{:S(2)}) collective-permute-start(bf16[128,768]{1,0:T(8,128)(2,1)S(1)} %get-tuple-element.96), channel_id=1, source_target_pairs={{0,2},{1,3},{2,0},{3,1},{4,6},{5,7},{6,4},{7,5},{8,10},{9,11},{10,... | collective-permute-start | bytes 589832 | tf_op jit(solution)/shard_map/ppermute | solution.py:28
  49.0 7.7 %collective-permute-start.14 = (bf16[128,768]{1,0:T(8,128)(2,1)S(1)}, bf16[128,768]{1,0:T(8,128)(2,1)S(1)}, u32[]{:S(2)}, u32[]{:S(2)}) collective-permute-start(bf16[128,768]{1,0:T(8,128)(2,1)S(1)} %get-tuple-element.56), channel_id=1, source_target_pairs={{0,4},{4,8},{8,12},{12,0},{1,5},{5,9},{9,13},{13,1},{2,6},{6,10},{... | collective-permute-start | bytes 589832 | tf_op jit(solution)/shard_map/ppermute | solution.py:24
  49.8 8.5 %collective-permute-start.10 = (bf16[128,768]{1,0:T(8,128)(2,1)S(1)}, bf16[128,768]{1,0:T(8,128)(2,1)S(1)}, u32[]{:S(2)}, u32[]{:S(2)}) collective-permute-start(bf16[128,768]{1,0:T(8,128)(2,1)S(1)} %collective-permute-done.9.x0.hidden), channel_id=1, source_target_pairs={{0,1},{1,0},{2,3},{3,2},{4,5},{5,4},{6,7},{7,6},{8,9},{9,8},{10,11... | collective-permute-start | bytes 589832 | tf_op jit(solution)/shard_map/ppermute | solution.py:28
  75.5 7.0 %collective-permute-start.20 = (bf16[128,768]{1,0:T(8,128)(2,1)S(1)}, bf16[128,768]{1,0:T(8,128)(2,1)S(1)}, u32[]{:S(2)}, u32[]{:S(2)}) collective-permute-start(bf16[128,768]{1,0:T(8,128)(2,1)S(1)} %get-tuple-element.95), channel_id=1, source_target_pairs={{0,2},{1,3},{2,0},{3,1},{4,6},{5,7},{6,4},{7,5},{8,10},{9,11},{10,... | collective-permute-start | bytes 589832 | tf_op jit(solution)/shard_map/ppermute | solution.py:28
  82.8 9.0 %collective-permute-start.22 = (bf16[128,768]{1,0:T(8,128)(2,1)S(1)}, bf16[128,768]{1,0:T(8,128)(2,1)S(1)}, u32[]{:S(2)}, u32[]{:S(2)}) collective-permute-start(bf16[128,768]{1,0:T(8,128)(2,1)S(1)} %get-tuple-element.63), channel_id=1, source_target_pairs={{0,4},{4,8},{8,12},{12,0},{1,5},{5,9},{9,13},{13,1},{2,6},{6,10},{... | collective-permute-start | bytes 589832 | tf_op jit(solution)/shard_map/ppermute | solution.py:24
  82.9 10.0 %collective-permute-start.26 = (bf16[128,768]{1,0:T(8,128)(2,1)S(1)}, bf16[128,768]{1,0:T(8,128)(2,1)S(1)}, u32[]{:S(2)}, u32[]{:S(2)}) collective-permute-start(bf16[128,768]{1,0:T(8,128)(2,1)S(1)} %get-tuple-element.94), channel_id=1, source_target_pairs={{0,2},{1,3},{2,0},{3,1},{4,6},{5,7},{6,4},{7,5},{8,10},{9,11},{10,... | collective-permute-start | bytes 589832 | tf_op jit(solution)/shard_map/ppermute | solution.py:28
  91.8 5.7 %collective-permute-start.24 = (bf16[128,768]{1,0:T(8,128)(2,1)S(1)}, bf16[128,768]{1,0:T(8,128)(2,1)S(1)}, u32[]{:S(2)}, u32[]{:S(2)}) collective-permute-start(bf16[128,768]{1,0:T(8,128)(2,1)S(1)} %collective-permute-done.22.x0.hidden), channel_id=1, source_target_pairs={{0,2},{1,3},{2,0},{3,1},{4,6},{5,7},{6,4},{7,5},{8,10},{9,11},{10,... | collective-permute-start | bytes 589832 | tf_op jit(solution)/shard_map/ppermute | solution.py:28
  93.1 7.7 %collective-permute-start.27 = (bf16[128,768]{1,0:T(8,128)(2,1)S(1)}, bf16[128,768]{1,0:T(8,128)(2,1)S(1)}, u32[]{:S(2)}, u32[]{:S(2)}) collective-permute-start(bf16[128,768]{1,0:T(8,128)(2,1)S(1)} %get-tuple-element.66), channel_id=1, source_target_pairs={{0,4},{4,8},{8,12},{12,0},{1,5},{5,9},{9,13},{13,1},{2,6},{6,10},{... | collective-permute-start | bytes 589832 | tf_op jit(solution)/shard_map/ppermute | solution.py:24
  93.4 8.4 %collective-permute-start.23 = (bf16[128,768]{1,0:T(8,128)(2,1)S(1)}, bf16[128,768]{1,0:T(8,128)(2,1)S(1)}, u32[]{:S(2)}, u32[]{:S(2)}) collective-permute-start(bf16[128,768]{1,0:T(8,128)(2,1)S(1)} %collective-permute-done.22.x0.hidden), channel_id=1, source_target_pairs={{0,1},{1,0},{2,3},{3,2},{4,5},{5,4},{6,7},{7,6},{8,9},{9,8},{10,11... | collective-permute-start | bytes 589832 | tf_op jit(solution)/shard_map/ppermute | solution.py:28
  119.6 7.0 %collective-permute-start.33 = (bf16[128,768]{1,0:T(8,128)(2,1)S(1)}, bf16[128,768]{1,0:T(8,128)(2,1)S(1)}, u32[]{:S(2)}, u32[]{:S(2)}) collective-permute-start(bf16[128,768]{1,0:T(8,128)(2,1)S(1)} %get-tuple-element.93), channel_id=1, source_target_pairs={{0,2},{1,3},{2,0},{3,1},{4,6},{5,7},{6,4},{7,5},{8,10},{9,11},{10,... | collective-permute-start | bytes 589832 | tf_op jit(solution)/shard_map/ppermute | solution.py:28
  126.9 9.3 %collective-permute-start.35 = (bf16[128,768]{1,0:T(8,128)(2,1)S(1)}, bf16[128,768]{1,0:T(8,128)(2,1)S(1)}, u32[]{:S(2)}, u32[]{:S(2)}) collective-permute-start(bf16[128,768]{1,0:T(8,128)(2,1)S(1)} %get-tuple-element.73), channel_id=1, source_target_pairs={{0,4},{4,8},{8,12},{12,0},{1,5},{5,9},{9,13},{13,1},{2,6},{6,10},{... | collective-permute-start | bytes 589832 | tf_op jit(solution)/shard_map/ppermute | solution.py:24
  128.9 8.3 %collective-permute-start.39 = (bf16[128,768]{1,0:T(8,128)(2,1)S(1)}, bf16[128,768]{1,0:T(8,128)(2,1)S(1)}, u32[]{:S(2)}, u32[]{:S(2)}) collective-permute-start(bf16[128,768]{1,0:T(8,128)(2,1)S(1)} %get-tuple-element.92), channel_id=1, source_target_pairs={{0,2},{1,3},{2,0},{3,1},{4,6},{5,7},{6,4},{7,5},{8,10},{9,11},{10,... | collective-permute-start | bytes 589832 | tf_op jit(solution)/shard_map/ppermute | solution.py:28
  136.3 5.7 %collective-permute-start.37 = (bf16[128,768]{1,0:T(8,128)(2,1)S(1)}, bf16[128,768]{1,0:T(8,128)(2,1)S(1)}, u32[]{:S(2)}, u32[]{:S(2)}) collective-permute-start(bf16[128,768]{1,0:T(8,128)(2,1)S(1)} %collective-permute-done.35.x0.refs_5_), channel_id=1, source_target_pairs={{0,2},{1,3},{2,0},{3,1},{4,6},{5,7},{6,4},{7,5},{8,10},{9,11},{10,... | collective-permute-start | bytes 589832 | tf_op jit(solution)/shard_map/ppermute | solution.py:28
  137.5 7.5 %collective-permute-start.40 = (bf16[128,768]{1,0:T(8,128)(2,1)S(1)}, bf16[128,768]{1,0:T(8,128)(2,1)S(1)}, u32[]{:S(2)}, u32[]{:S(2)}) collective-permute-start(bf16[128,768]{1,0:T(8,128)(2,1)S(1)} %get-tuple-element.76), channel_id=1, source_target_pairs={{0,4},{4,8},{8,12},{12,0},{1,5},{5,9},{9,13},{13,1},{2,6},{6,10},{... | collective-permute-start | bytes 589832 | tf_op jit(solution)/shard_map/ppermute | solution.py:24
  137.6 9.6 %collective-permute-start.36 = (bf16[128,768]{1,0:T(8,128)(2,1)S(1)}, bf16[128,768]{1,0:T(8,128)(2,1)S(1)}, u32[]{:S(2)}, u32[]{:S(2)}) collective-permute-start(bf16[128,768]{1,0:T(8,128)(2,1)S(1)} %collective-permute-done.35.x0.refs_5_), channel_id=1, source_target_pairs={{0,1},{1,0},{2,3},{3,2},{4,5},{5,4},{6,7},{7,6},{8,9},{9,8},{10,11... | collective-permute-start | bytes 589832 | tf_op jit(solution)/shard_map/ppermute | solution.py:28
  146.1 9.1 %collective-permute-start.44 = (bf16[256,768]{1,0:T(8,128)(2,1)S(1)}, bf16[256,768]{1,0:T(8,128)(2,1)S(1)}, u32[]{:S(2)}, u32[]{:S(2)}) collective-permute-start(bf16[256,768]{1,0:T(8,128)(2,1)S(1)} %pad_maximum_fusion), channel_id=1, source_target_pairs={{12,8},{13,9},{14,10},{15,11},{28,24},{29,25},{30,26},{31,27}} | collective-permute-start | bytes 1179656 | tf_op jit(solution)/shard_map/ppermute | solution.py:373
  163.1 13.7 %collective-permute-start.55 = (bf16[256,768]{1,0:T(8,128)(2,1)S(1)}, bf16[256,768]{1,0:T(8,128)(2,1)S(1)}, u32[]{:S(2)}, u32[]{:S(2)}) collective-permute-start(bf16[256,768]{1,0:T(8,128)(2,1)S(1)} %pad_maximum_fusion.1), channel_id=1, source_target_pairs={{12,4},{13,5},{14,6},{15,7},{28,20},{29,21},{30,22},{31,23}} | collective-permute-start | bytes 1179656 | tf_op jit(solution)/shard_map/ppermute | solution.py:373
  164.3 5.7 %collective-permute-start.53 = (bf16[64,768]{1,0:T(8,128)(2,1)S(1)}, bf16[64,768]{1,0:T(8,128)(2,1)S(1)}, u32[]{:S(2)}, u32[]{:S(2)}) collective-permute-start(bf16[64,768]{1,0:T(8,128)(2,1)S(1)} %get-tuple-element.88), channel_id=1, source_target_pairs={{0,2},{1,3},{2,0},{3,1},{4,6},{5,7},{6,4},{7,5},{8,10},{9,11},{10,... | collective-permute-start | bytes 294920 | tf_op jit(solution)/shard_map/ppermute | solution.py:28
  165.4 6.7 %collective-permute-start.51 = (bf16[64,768]{1,0:T(8,128)(2,1)S(1)}, bf16[64,768]{1,0:T(8,128)(2,1)S(1)}, u32[]{:S(2)}, u32[]{:S(2)}) collective-permute-start(bf16[64,768]{1,0:T(8,128)(2,1)S(1)} %get-tuple-element.89), channel_id=1, source_target_pairs={{0,2},{1,3},{2,0},{3,1},{4,6},{5,7},{6,4},{7,5},{8,10},{9,11},{10,... | collective-permute-start | bytes 294920 | tf_op jit(solution)/shard_map/ppermute | solution.py:28
  166.4 7.9 %collective-permute-start.49 = (bf16[64,768]{1,0:T(8,128)(2,1)S(1)}, bf16[64,768]{1,0:T(8,128)(2,1)S(1)}, u32[]{:S(2)}, u32[]{:S(2)}) collective-permute-start(bf16[64,768]{1,0:T(8,128)(2,1)S(1)} %get-tuple-element.90), channel_id=1, source_target_pairs={{0,2},{1,3},{2,0},{3,1},{4,6},{5,7},{6,4},{7,5},{8,10},{9,11},{10,... | collective-permute-start | bytes 294920 | tf_op jit(solution)/shard_map/ppermute | solution.py:28
  167.4 8.1 %collective-permute-start.47 = (bf16[64,768]{1,0:T(8,128)(2,1)S(1)}, bf16[64,768]{1,0:T(8,128)(2,1)S(1)}, u32[]{:S(2)}, u32[]{:S(2)}) collective-permute-start(bf16[64,768]{1,0:T(8,128)(2,1)S(1)} %get-tuple-element.91), channel_id=1, source_target_pairs={{0,2},{1,3},{2,0},{3,1},{4,6},{5,7},{6,4},{7,5},{8,10},{9,11},{10,... | collective-permute-start | bytes 294920 | tf_op jit(solution)/shard_map/ppermute | solution.py:28
  170.2 8.9 %collective-permute-start.54 = (bf16[64,768]{1,0:T(8,128)(2,1)S(1)}, bf16[64,768]{1,0:T(8,128)(2,1)S(1)}, u32[]{:S(2)}, u32[]{:S(2)}) collective-permute-start(bf16[64,768]{1,0:T(8,128)(2,1)S(1)} %update.19), channel_id=1, source_target_pairs={{0,4},{4,8},{8,12},{12,0},{1,5},{5,9},{9,13},{13,1},{2,6},{6,10},{... | collective-permute-start | bytes 294920 | tf_op jit(solution)/shard_map/ppermute | solution.py:24
  172.3 8.9 %collective-permute-start.52 = (bf16[64,768]{1,0:T(8,128)(2,1)S(1)}, bf16[64,768]{1,0:T(8,128)(2,1)S(1)}, u32[]{:S(2)}, u32[]{:S(2)}) collective-permute-start(bf16[64,768]{1,0:T(8,128)(2,1)S(1)} %update.18), channel_id=1, source_target_pairs={{0,4},{4,8},{8,12},{12,0},{1,5},{5,9},{9,13},{13,1},{2,6},{6,10},{... | collective-permute-start | bytes 294920 | tf_op jit(solution)/shard_map/ppermute | solution.py:24
  174.4 8.9 %collective-permute-start.50 = (bf16[64,768]{1,0:T(8,128)(2,1)S(1)}, bf16[64,768]{1,0:T(8,128)(2,1)S(1)}, u32[]{:S(2)}, u32[]{:S(2)}) collective-permute-start(bf16[64,768]{1,0:T(8,128)(2,1)S(1)} %update.17), channel_id=1, source_target_pairs={{0,4},{4,8},{8,12},{12,0},{1,5},{5,9},{9,13},{13,1},{2,6},{6,10},{... | collective-permute-start | bytes 294920 | tf_op jit(solution)/shard_map/ppermute | solution.py:24
  175.7 9.3 %collective-permute-start.48 = (bf16[64,768]{1,0:T(8,128)(2,1)S(1)}, bf16[64,768]{1,0:T(8,128)(2,1)S(1)}, u32[]{:S(2)}, u32[]{:S(2)}) collective-permute-start(bf16[64,768]{1,0:T(8,128)(2,1)S(1)} %update.16), channel_id=1, source_target_pairs={{0,4},{4,8},{8,12},{12,0},{1,5},{5,9},{9,13},{13,1},{2,6},{6,10},{... | collective-permute-start | bytes 294920 | tf_op jit(solution)/shard_map/ppermute | solution.py:24
  (33 other events, 132.6 us)
